TPU v7x, 32 devices: a whole 2x2x4 slice. The times are simulated.
32 devices in a mesh: seq: 8 (over z, x), tp: 4 (over y, core).
Axes of the slice: x: 2, y: 2, z: 4, core: 2. Of those that a mesh axis runs over, the one named last changes fastest.
Arguments:
- draft_q: bfloat16 [256, 4096], P('seq', 'tp'), may hold values from -16 to 16
- draft_kv: bfloat16 [2, 256, 4096], P(None, 'seq', 'tp'), may hold values from -6 to 6
- kv_pool: bfloat16 [2, 128, 128, 4096], P(None, 'seq', None, 'tp'), may hold values from -8 to 8
- page_table: int32 [4, 32], replicated, may hold values from -1 to 127, as said below
- cache_len: int32 [4], replicated, may hold values from 2048 to 4096, as said below
- tree_mask: int32 [4, 64, 64], replicated, may hold values from 0 to 1, as said below
- accepted_rows: int32 [4, 64], replicated, may hold values from -1 to 63, as said below
- out_weight: bfloat16 [4096, 4096], P('tp'), may hold values from -0.125 to 0.125
Outputs:
- layer_out: bfloat16 [256, 4096], P('seq', 'tp')
- accepted_kv: bfloat16 [2, 4, 128, 4096], P(None, None, None, 'tp')
Inputs may be any that keep to these rules, and one draw needn't show every extreme that they name: `page_table`: entries past a request's cached pages are -1; the slots in use are distinct over all requests. `cache_len`: some request holds exactly 4096 cached tokens. `tree_mask`: entry (r, i, k) is 1 where draft row k is row i itself or one of its ancestors in request r's token tree; a parent precedes its children, row 0 is the root. `accepted_rows`: each row lists in ascending order the draft rows of one root-to-node path of the tree, then -1.
All inputs are finite; a program needn't handle non-finite values.
Results may differ from a plain program's by a relative error of at most 0.0051.
Values may be sent and summed in bfloat16 or wider, within the bound.
A program may use at most 128 MiB of HBM per device.

v0:
```python
import math

import jax
import jax.numpy as jnp
from jax import lax
from jax.sharding import PartitionSpec as P

HD = 128


NEGATIVE = -1e30


def body(draft_q, draft_kv, kv_pool, page_table, cache_len, tree_mask, accepted_rows, out_weight):
    inv_root = 1.0 / math.sqrt(HD)
    highest = lax.Precision.HIGHEST
    n_seq = lax.axis_size("seq")
    rows_dev = draft_q.shape[0]
    width_loc = draft_q.shape[1]
    heads_loc = width_loc // HD
    n_req = page_table.shape[0]
    n_pages = page_table.shape[1]
    n_draft = tree_mask.shape[1]
    n_slots = kv_pool.shape[1]
    page_len = kv_pool.shape[2]
    rows_all = rows_dev * n_seq
    query_all, kv_all = (
        lax.all_gather(draft_q, "seq", axis=0, tiled=True),
        lax.all_gather(draft_kv, "seq", axis=1, tiled=True),
    )
    first_slot = lax.axis_index("seq") * n_slots
    slot_ids = first_slot + jnp.arange(n_slots, dtype=jnp.int32)
    slot_hits = page_table[None, :, :] == slot_ids[:, None, None]
    owner_hot = jnp.any(slot_hits, axis=2)
    is_live = jnp.any(owner_hot, axis=1)
    owner_req = jnp.sum(owner_hot * jnp.arange(n_req, dtype=jnp.int32)[None, :], axis=1)
    logical = jnp.sum(slot_hits * jnp.arange(n_pages, dtype=jnp.int32)[None, None, :], axis=(1, 2))
    len_limit = jnp.sum(owner_hot * cache_len[None, :], axis=1)
    positions = logical[:, None] * page_len + jnp.arange(page_len, dtype=jnp.int32)[None, :]
    is_valid = is_live[:, None] & (positions < len_limit[:, None])
    query_req = query_all.reshape(n_req, n_draft, heads_loc, HD)
    page_query = query_req[owner_req]
    page_keys = kv_pool[0].reshape(n_slots, page_len, heads_loc, HD)
    page_values = kv_pool[1].reshape(n_slots, page_len, heads_loc, HD)
    scores = (
        jnp.einsum("sqhd,sthd->shqt", page_query, page_keys, preferred_element_type=jnp.float32)
        * inv_root
    )
    allowed = is_valid[:, None, None, :]
    masked = jnp.where(allowed, scores, NEGATIVE)
    page_max = jnp.max(masked, axis=3)
    weights = jnp.where(allowed, jnp.exp(masked - page_max[..., None]), 0.0)
    page_total = jnp.sum(weights, axis=3)
    page_out = jnp.einsum(
        "shqt,sthd->shqd",
        weights.astype(jnp.bfloat16),
        page_values,
        preferred_element_type=jnp.float32,
    )
    req_max = jnp.max(
        jnp.where(owner_hot[:, :, None, None], page_max[:, None, :, :], NEGATIVE), axis=0
    )
    weight = jnp.exp(page_max - req_max[owner_req])
    own_hot = owner_hot.astype(jnp.float32)
    local_total = jnp.einsum(
        "sr,shq->rqh", own_hot, weight * page_total, precision=highest
    ).reshape(rows_all, heads_loc)
    local_out = jnp.einsum(
        "sr,shqd->rqhd", own_hot, weight[..., None] * page_out, precision=highest
    ).reshape(rows_all, width_loc)
    local_max = jnp.transpose(req_max, (0, 2, 1)).reshape(rows_all, heads_loc)
    row_start = lax.axis_index("seq") * rows_dev
    got_max, got_total, got_out = (
        lax.all_to_all(local_max, "seq", split_axis=0, concat_axis=0, tiled=True),
        lax.all_to_all(local_total, "seq", split_axis=0, concat_axis=0, tiled=True),
        lax.all_to_all(local_out, "seq", split_axis=0, concat_axis=0, tiled=True),
    )
    got_max = got_max.reshape(n_seq, rows_dev, heads_loc)
    own_max = jnp.max(got_max, axis=0)
    factor = jnp.exp(got_max - own_max[None])
    own_total = jnp.sum(got_total.reshape(n_seq, rows_dev, heads_loc) * factor, axis=0)
    own_out = jnp.sum(got_out.reshape(n_seq, rows_dev, heads_loc, HD) * factor[..., None], axis=0)
    own_query = draft_q.reshape(rows_dev, heads_loc, HD)
    tree_keys = kv_all[0].reshape(rows_all, heads_loc, HD)
    tree_values = kv_all[1].reshape(rows_all, heads_loc, HD)
    ancestry = tree_mask.reshape(rows_all, n_draft)
    own_ancestry = lax.dynamic_slice_in_dim(ancestry, row_start, rows_dev, 0)
    row_req = (row_start + jnp.arange(rows_dev, dtype=jnp.int32)) // n_draft
    key_req = jnp.arange(rows_all, dtype=jnp.int32) // n_draft
    tree_allowed = (jnp.tile(own_ancestry, (1, n_req)) == 1) & (
        row_req[:, None] == key_req[None, :]
    )
    tree_scores = (
        jnp.einsum("qhd,khd->hqk", own_query, tree_keys, preferred_element_type=jnp.float32)
        * inv_root
    )
    tree_masked = jnp.where(tree_allowed[None], tree_scores, NEGATIVE)
    tree_max = jnp.max(tree_masked, axis=2)
    tree_weights = jnp.where(tree_allowed[None], jnp.exp(tree_masked - tree_max[..., None]), 0.0)
    tree_total = jnp.transpose(jnp.sum(tree_weights, axis=2))
    tree_out = jnp.einsum(
        "hqk,khd->qhd",
        tree_weights.astype(jnp.bfloat16),
        tree_values,
        preferred_element_type=jnp.float32,
    )
    tree_max = jnp.transpose(tree_max)
    row_top = jnp.maximum(own_max, tree_max)
    cache_factor = jnp.exp(own_max - row_top)
    tree_factor = jnp.exp(tree_max - row_top)
    numerator = own_out * cache_factor[..., None] + tree_out * tree_factor[..., None]
    denominator = own_total * cache_factor + tree_total * tree_factor
    attention = (
        (numerator / denominator[..., None]).reshape(rows_dev, width_loc).astype(jnp.bfloat16)
    )
    partial_value = jnp.dot(attention, out_weight, preferred_element_type=jnp.float32)
    layer_out = lax.psum_scatter(partial_value, "tp", scatter_dimension=1, tiled=True).astype(
        jnp.bfloat16
    )
    picked = jnp.concatenate(
        [accepted_rows, jnp.full((n_req, page_len - n_draft), -1, jnp.int32)], axis=1
    )
    onehot = (picked[:, :, None] == jnp.arange(n_draft, dtype=jnp.int32)[None, None, :]).astype(
        jnp.bfloat16
    )
    kv_blocks = kv_all.reshape(2, n_req, n_draft, width_loc)
    accepted_kv = jnp.einsum(
        "rji,crid->crjd", onehot, kv_blocks, preferred_element_type=jnp.float32
    ).astype(jnp.bfloat16)
    return (layer_out, accepted_kv)


def solution(mesh):
    return jax.shard_map(
        body,
        mesh=mesh,
        in_specs=(
            P("seq", "tp"),
            P(None, "seq", "tp"),
            P(None, "seq", None, "tp"),
            P(),
            P(),
            P(),
            P(),
            P("tp", None),
        ),
        out_specs=(P("seq", "tp"), P(None, None, None, "tp")),
        check_vma=False,
    )
```

profile of v0, /device:TPU:11, one launch (start us, length us, event | category | flops | bytes accessed | tf_op | source)
XLA Modules:
  0.0 170.8 jit_solution(13782191911061992662)
XLA Ops:
  7.2 1.0 compare_reduce_fusion.1
  8.2 0.9 fusion.38
  9.2 0.7 select_reduce_fusion.2
  9.9 23.3 %all_gather.6 = bf16[256,1024]{1,0:T(8,128)(2,1)S(1)} all-gather(bf16[32,1024]{1,0:T(8,128)(2,1)} %param.8), channel_id=1, replica_groups=mesh['seq'=8,'tp'=4] {'seq'}, dimensions={0}, use_global_device_ids=true | all-gather | bytes 589824 | tf_op jit(solution)/shard_map/all_gather | solution.py:28
  33.3 6.0 %fusion.53 = (bf16[1,16,128,1024]{3,2,1,0:T(8,128)(2,1)}, bf16[1,16,128,1024]{3,2,1,0:T(8,128)(2,1)}) fusion(bf16[2,16,128,1024]{3,2,1,0:T(8,128)(2,1)} %param.10), kind=kLoop, calls=%fused_computation.86 | loop fusion | bytes 16777216 | tf_op jit(solution)/shard_map/slice | solution.py:43
  39.3 6.4 %copy.128 = bf16[1,16,128,1024]{2,3,1,0:T(8,128)(2,1)} copy(bf16[1,16,128,1024]{3,2,1,0:T(8,128)(2,1)} %get-tuple-element.25) | data formatting | bytes 8388608
  45.7 0.9 gather_fusion
  46.7 3.5 %fusion.2 = (f32[16,8,64]{2,1,0:T(8,128)S(1)}, f32[16,8,64,128]{3,2,1,0:T(8,128)S(1)}) fusion(pred[16,128]{1,0:T(8,128)(4,1)S(1)} %fusion.39, bf16[16,128,8,128]{1,3,2,0:T(8,128)(2,1)} %bitcast.99, bf16[16,64,8,128]{3,2,1,0:T(8,128)(2,1)S(1)} %gather_fusion), kind=kOutput, calls=%fused_computation.6 | convolution fusion | flops 271572992 | bytes 10520576 | tf_op jit(solution)/shard_map/sqhd,sthd->shqt/dot_general | solution.py:46
  50.3 1.9 %copy-done = f32[16,8,64,128]{3,2,1,0:T(8,128)} copy-done((f32[16,8,64,128]{3,2,1,0:T(8,128)}, f32[16,8,64,128]{3,2,1,0:T(8,128)S(1)}, u32[]{:S(2)}) %copy-start) | copy-done | bytes 4194328
  52.2 2.4 %fusion.3 = f32[16,8,64]{2,1,0:T(8,128)S(1)} fusion(f32[16,8,64,128]{3,2,1,0:T(8,128)S(1)} %get-tuple-element.30, f32[16,8,64]{2,1,0:T(8,128)S(1)} %get-tuple-element.29, pred[16,128]{1,0:T(8,128)(4,1)S(1)} %fusion.39), kind=kLoop, calls=%fused_computation.7 | loop fusion | flops 5234688 | bytes 4261888 | tf_op jit(solution)/shard_map/reduce_sum | solution.py:53
  55.6 0.7 reshape.220
  56.3 8.0 %all-to-all-start.2 = ((f32[8,1,256]{2,1,0:T(1,128)}), f32[8,1,256]{2,1,0:T(1,128)S(1)}, u32[]{:S(2)}, u32[]{:S(2)}) async-start(f32[8,1,256]{2,1,0:T(1,128)} %reshape.220), calls=%async_computation.2 | async-start | bytes 16384 | tf_op jit(solution)/shard_map/all_to_all | solution.py:75
  64.3 0.8 copy.107
  65.1 6.4 %copy.129 = bf16[1,16,128,1024]{2,3,1,0:T(8,128)(2,1)} copy(bf16[1,16,128,1024]{3,2,1,0:T(8,128)(2,1)} %get-tuple-element.26) | data formatting | bytes 8388608
  71.5 6.6 %convolution_multiply_fusion = f32[16,8,64,128]{3,2,1,0:T(8,128)} fusion(bf16[16,128,8,128]{1,3,2,0:T(8,128)(2,1)} %bitcast.100, f32[16,8,64,128]{3,2,1,0:T(8,128)} %copy-done, f32[16,8,64]{2,1,0:T(8,128)S(1)} %get-tuple-element.29, f32[16,8,64]{2,1,0:T(8,128)S(1)} %get-tuple-element.24, pred[16,128]{1,0:T(8,128)(4,1)S(1)} %fusion.39), kind=kOutput, calls=%fused_computation.9 | convolution fusion | flops 274726912 | bytes 12650496 | tf_op jit(solution)/shard_map/shqt,sthd->shqd/dot_general | solution.py:54
  78.2 0.7 reshape.218
  78.9 5.4 %all-to-all-start.1 = ((f32[8,1,256]{2,1,0:T(1,128)}), f32[8,1,256]{2,1,0:T(1,128)S(1)}, u32[]{:S(2)}, u32[]{:S(2)}) async-start(f32[8,1,256]{2,1,0:T(1,128)} %reshape.218), calls=%async_computation.1 | async-start | bytes 16384 | tf_op jit(solution)/shard_map/all_to_all | solution.py:74
  84.3 5.9 %fusion.13 = f32[4,64,8,128]{3,0,1,2:T(4,128)S(1)} fusion(f32[16,8,64,128]{3,2,1,0:T(8,128)} %convolution_multiply_fusion, pred[16,4]{0,1:T(4,128)(4,1)S(1)} %get-tuple-element.15), kind=kOutput, calls=%fused_computation.18 | convolution fusion | flops 50331648 | bytes 5242944 | tf_op jit(solution)/shard_map/sr,shqd->rqhd/dot_general | solution.py:68
  90.9 1.1 all_to_all.18
  92.0 5.4 %all-to-all-start = ((f32[8,32,1024]{2,1,0:T(8,128)}), f32[8,32,1024]{2,1,0:T(8,128)S(1)}, u32[]{:S(2)}, u32[]{:S(2)}) async-start(f32[8,32,1024]{2,1,0:T(8,128)} %all_to_all.18), calls=%async_computation | async-start | bytes 2097152 | tf_op jit(solution)/shard_map/all_to_all | solution.py:76
  97.5 0.7 dynamic-slice_compare_fusion
  101.1 19.1 %all-gather.2.cloned.1.call-done = bf16[2,256,1024]{2,0,1:T(2,128)(2,1)} async-done(((bf16[2,32,1024]{2,0,1:T(2,128)(2,1)}), bf16[2,256,1024]{2,0,1:T(2,128)(2,1)}) %all-gather.2.cloned.1.call-update) | async-done | bytes 1048592 | tf_op jit(solution)/shard_map/all_gather | solution.py:29
  120.1 4.1 %fusion.54 = (bf16[1,256,1024]{2,0,1:T(2,128)(2,1)}, bf16[1,256,1024]{2,0,1:T(2,128)(2,1)S(1)}) fusion(bf16[2,256,1024]{2,0,1:T(2,128)(2,1)} %all-gather.2.cloned.1.call-done), kind=kLoop, calls=%fused_computation.87 | loop fusion | bytes 2097152 | tf_op jit(solution)/shard_map/slice | solution.py:84
  124.2 3.5 %copy.130 = bf16[1,256,1024]{1,2,0:T(8,128)(2,1)} copy(bf16[1,256,1024]{2,0,1:T(2,128)(2,1)} %get-tuple-element.27) | data formatting | bytes 1048576
  127.7 2.0 %copy.131 = bf16[1,256,1024]{1,2,0:T(8,128)(2,1)} copy(bf16[1,256,1024]{2,0,1:T(2,128)(2,1)S(1)} %get-tuple-element.28) | data formatting | bytes 1048576
  129.7 1.3 fusion.55
  131.4 1.4 fusion.21
  132.8 5.8 %fusion.31 = f32[32,4096]{1,0:T(8,128)} fusion(bf16[1024,4096]{1,0:T(8,128)(2,1)} %param.15, bf16[8,4,8,128]{3,2,1,0:T(8,128)(2,1)S(1)} %fusion.21), kind=kOutput, calls=%fused_computation.40 | convolution fusion | flops 268435456 | bytes 8978432 | tf_op jit(solution)/shard_map/dot_general | solution.py:116
  138.7 0.8 convert_bitcast_fusion
  139.4 1.5 copy.119
  140.9 21.5 %reduce-scatter.2.cloned.1.call-done = f32[32,1024]{1,0:T(8,128)} async-done(((f32[32,4096]{1,0:T(8,128)}), f32[32,1024]{1,0:T(8,128)}) %reduce-scatter.2.cloned.1.call-update) | async-done | bytes 131088 | tf_op jit(solution)/shard_map/reduce_scatter | solution.py:117
  162.4 1.5 convert_element_type.30
  (52 shorter events, 5.2 us)
Async XLA Ops:
  50.2 2.0 %copy-start = (f32[16,8,64,128]{3,2,1,0:T(8,128)}, f32[16,8,64,128]{3,2,1,0:T(8,128)S(1)}, u32[]{:S(2)}) copy-start(f32[16,8,64,128]{3,2,1,0:T(8,128)S(1)} %get-tuple-element.30) | copy-start | bytes 12582916
  50.3 14.0 %copy-start.3 = (bf16[2,32,1024]{2,1,0:T(8,128)(2,1)S(1)}, bf16[2,32,1024]{2,1,0:T(8,128)(2,1)}, u32[]{:S(2)}) copy-start(bf16[2,32,1024]{2,1,0:T(8,128)(2,1)} %param.9) | copy-start | bytes 393220
  56.3 22.6 %all-to-all-start.2 = ((f32[8,1,256]{2,1,0:T(1,128)}), f32[8,1,256]{2,1,0:T(1,128)S(1)}, u32[]{:S(2)}, u32[]{:S(2)}) async-start(f32[8,1,256]{2,1,0:T(1,128)} %reshape.220), calls=%async_computation.2 | async-start | bytes 16384 | tf_op jit(solution)/shard_map/all_to_all | solution.py:75
  64.3 55.9 %all-gather.2.cloned.1.call-start = ((), (), s32[]{:S(2)}) async-start(), calls=%async_computation.4 | async-start | bytes 1179648 | tf_op jit(solution)/shard_map/all_gather | solution.py:29
  78.9 13.1 %all-to-all-start.1 = ((f32[8,1,256]{2,1,0:T(1,128)}), f32[8,1,256]{2,1,0:T(1,128)S(1)}, u32[]{:S(2)}, u32[]{:S(2)}) async-start(f32[8,1,256]{2,1,0:T(1,128)} %reshape.218), calls=%async_computation.1 | async-start | bytes 16384 | tf_op jit(solution)/shard_map/all_to_all | solution.py:74
  92.0 39.2 %all-to-all-start = ((f32[8,32,1024]{2,1,0:T(8,128)}), f32[8,32,1024]{2,1,0:T(8,128)S(1)}, u32[]{:S(2)}, u32[]{:S(2)}) async-start(f32[8,32,1024]{2,1,0:T(8,128)} %all_to_all.18), calls=%async_computation | async-start | bytes 2097152 | tf_op jit(solution)/shard_map/all_to_all | solution.py:76
  97.5 65.0 %reduce-scatter.2.cloned.1.call-start = ((), (), s32[]{:S(2)}) async-start(), calls=%async_computation.5 | async-start | bytes 655360 | tf_op jit(solution)/shard_map/reduce_scatter | solution.py:117
  101.1 28.6 %copy-start.2 = (bf16[32,1024]{1,0:T(8,128)(2,1)S(1)}, bf16[32,1024]{1,0:T(8,128)(2,1)}, u32[]{:S(2)}) copy-start(bf16[32,1024]{1,0:T(8,128)(2,1)} %param.8) | copy-start | bytes 196612
  132.8 5.9 %copy-start.4 = (s32[4,64]{1,0:T(4,128)S(1)}, s32[4,64]{1,0:T(4,128)}, u32[]{:S(2)}) copy-start(s32[4,64]{1,0:T(4,128)} %param.14) | copy-start | bytes 3076
  132.8 5.9 %copy-start.1 = (bf16[2,256,1024]{2,0,1:T(2,128)(2,1)S(1)}, bf16[2,256,1024]{2,0,1:T(2,128)(2,1)}, u32[]{:S(2)}) copy-start(bf16[2,256,1024]{2,0,1:T(2,128)(2,1)} %all-gather.2.cloned.1.call-done) | copy-start | bytes 3145732
Sparse Core Ops, SparseCore 0:
  67.8 52.2 all-gather.1
  138.8 23.6 reduce-scatter.1
where the time goes:
time: 173 us; the launch traced here: 171 us
  waiting for transfers between devices  40.6 us (23%)
  local copies, waits for them, and re-layouts  38.9 us (22%)
  matrix products  25.5 us (15%)
  blocking collectives  23.3 us (13%)
  starting transfers between devices  18.8 us (11%)
  between operations  14.3 us (8%)
  other arithmetic  9.36 us (5%)
    unnamed x21, local copies, waits for them, and re-layouts  24 us
    all_gather x1, blocking collectives, body(): lax.all_gather(draft_q, 'seq', axis=0, tiled=True)  23.3 us
    reduce_scatter x1, waiting for transfers between devices, body(): lax.psum_scatter(partial_value, 'tp', scatter_dimension=1, tiled=True)  21.5 us
    all_gather x1, waiting for transfers between devices, body(): lax.all_gather(draft_kv, 'seq', axis=1, tiled=True)  19.1 us
    all_to_all x1, starting transfers between devices, body(): lax.all_to_all(local_total, 'seq', split_axis=0, concat_axis=0, tiled=True)  7.96 us
    dot_general x1, matrix products, body(): jnp.einsum('shqt,sthd->shqd', weights.astype(jnp.bfloat16), page_values,...  6.64 us
    slice x1, local copies, waits for them, and re-layouts, body(): page_keys = kv_pool[0].reshape(n_slots, page_len, heads_loc, HD)  6.01 us
    dot_general x1, matrix products, body(): jnp.einsum('sr,shqd->rqhd', own_hot, weight[..., None] * page_out, precis...  5.91 us
  transfers between devices with their start and end apart: 5, of which 2 were waited for; matrix products, arithmetic and copies ran while one was open for 22% of the time, Pallas kernels for 0%

commit v1 on v0

v1 whole, which is shorter than its diff:
```python
import functools
import math

import jax
import jax.numpy as jnp
from jax import lax
from jax.experimental import pallas as pl
from jax.experimental.pallas import tpu as pltpu
from jax.sharding import PartitionSpec as P

HD = 128
NEGATIVE = -1e30
MESH = pl.DeviceIdType.MESH
ANY = pl.BlockSpec(memory_space=pl.ANY)
VMEM = pl.BlockSpec(memory_space=pltpu.VMEM)
SMEM = pl.BlockSpec(memory_space=pltpu.SMEM)
NT = (((1,), (1,)), ((), ()))


def gather_kernel(n_req, group, q, kv, qa, kg, ssem, rsem, fsem, kssem, krsem, lsem):
    me = lax.axis_index("seq")
    grp = me // group
    inner = lax.rem(me, group)

    def across(d):
        return lax.rem(grp + d, n_req) * group + inner

    def mate(d):
        return lax.rem(inner + d, group)

    def other(d):
        return grp * group + mate(d)

    barrier = pltpu.get_barrier_semaphore()
    for d in range(1, n_req):
        pl.semaphore_signal(barrier, inc=1, device_id={"seq": across(d)}, device_id_type=MESH)
    for d in range(1, group):
        pl.semaphore_signal(barrier, inc=1, device_id={"seq": other(d)}, device_id_type=MESH)
    own_q = pltpu.make_async_copy(q, qa.at[me], lsem.at[0])
    own_kv = pltpu.make_async_copy(kv, kg.at[inner], lsem.at[1])
    own_q.start()
    own_kv.start()
    pl.semaphore_wait(barrier, n_req + group - 2)

    def send(src, dst, s, r, target):
        c = pltpu.make_async_remote_copy(
            src_ref=src, dst_ref=dst, send_sem=s, recv_sem=r,
            device_id={"seq": target}, device_id_type=MESH)
        c.start()
        return c

    sent = []
    for d in range(1, n_req):
        sent.append(send(q, qa.at[me], ssem.at[d - 1], rsem.at[me], across(d)))
    for d in range(1, group):
        sent.append(send(q, qa.at[me], ssem.at[n_req - 2 + d], rsem.at[me], other(d)))
    for d in range(1, group):
        sent.append(send(kv, kg.at[inner], kssem.at[d - 1], krsem.at[inner], other(d)))

    def arrived(b):
        pltpu.make_async_remote_copy(
            src_ref=q, dst_ref=qa.at[b], send_sem=ssem.at[0], recv_sem=rsem.at[b],
            device_id={"seq": other(1)}, device_id_type=MESH).wait_recv()

    for e in range(1, n_req):
        b = across(n_req - e)
        arrived(b)
        for d in range(1, group):
            sent.append(send(qa.at[b], qa.at[b], fsem.at[(e - 1) * (group - 1) + d - 1],
                             rsem.at[b], other(d)))
    for d in range(1, group):
        arrived(other(d))
        m = mate(d)
        pltpu.make_async_remote_copy(
            src_ref=kv, dst_ref=kg.at[m], send_sem=kssem.at[0], recv_sem=krsem.at[m],
            device_id={"seq": other(1)}, device_id_type=MESH).wait_recv()
        for e in range(1, n_req):
            arrived(lax.rem(grp + e, n_req) * group + m)
    for c in sent:
        c.wait_send()
    own_q.wait()
    own_kv.wait()


def page_kernel(page_table, cache_len, first, qa, pool, acc_out, stat_out,
                kbuf, vbuf, m_ref, l_ref, acc, owner, limit, ksem, vsem):
    n_slots, page_len, width = kbuf.shape
    heads = width // HD
    n_req, n_pages = page_table.shape
    for s in range(n_slots):
        pltpu.make_async_copy(pool.at[0, s], kbuf.at[s], ksem.at[s]).start()
        pltpu.make_async_copy(pool.at[1, s], vbuf.at[s], vsem.at[s]).start()
    m_ref[...] = jnp.full(m_ref.shape, NEGATIVE, jnp.float32)
    l_ref[...] = jnp.zeros(l_ref.shape, jnp.float32)
    acc[...] = jnp.zeros(acc.shape, jnp.float32)
    for s in range(n_slots):
        owner[s] = 0
        limit[s] = 0
    base = first[0]
    for r in range(n_req):
        length = cache_len[r]
        for j in range(n_pages):
            slot = page_table[r, j] - base

            @pl.when((page_table[r, j] >= 0) & (slot >= 0) & (slot < n_slots))
            def _():
                owner[slot] = r
                limit[slot] = length - j * page_len

    scale = 1.0 / math.sqrt(HD)

    def step(s, carry):
        pltpu.make_async_copy(pool.at[0, s], kbuf.at[s], ksem.at[s]).wait()
        pltpu.make_async_copy(pool.at[1, s], vbuf.at[s], vsem.at[s]).wait()
        left = limit[s]

        @pl.when(left > 0)
        def _():
            r = owner[s]
            scores = []
            for h in range(heads):
                cols = slice(h * HD, (h + 1) * HD)
                scores.append(lax.dot_general(
                    qa[r, :, cols], kbuf[s, :, cols], NT, preferred_element_type=jnp.float32))
            live = lax.broadcasted_iota(jnp.int32, scores[0].shape, 1) < left
            probs = []
            scales = []
            for h in range(heads):
                x = jnp.where(live, scores[h] * scale, NEGATIVE)
                old = m_ref[r, h]
                new = jnp.maximum(old, jnp.max(x, axis=1, keepdims=True))
                p = jnp.exp(x - new)
                a = jnp.exp(old - new)
                m_ref[r, h] = new
                l_ref[r, h] = a * l_ref[r, h] + jnp.sum(p, axis=1, keepdims=True)
                probs.append(p.astype(jnp.bfloat16))
                scales.append(a)
            for h in range(heads):
                cols = slice(h * HD, (h + 1) * HD)
                o = jnp.dot(probs[h], vbuf[s, :, cols], preferred_element_type=jnp.float32)
                acc[r, :, cols] = scales[h] * acc[r, :, cols] + o

        return carry

    lax.fori_loop(0, n_slots, step, 0)
    acc_out[...] = acc[...].astype(jnp.bfloat16)
    n_draft = acc.shape[1]
    lane = lax.broadcasted_iota(jnp.int32, (n_draft, HD), 1)
    for r in range(n_req):
        stat = jnp.zeros((n_draft, HD), jnp.float32)
        for h in range(heads):
            stat = jnp.where(lane == h, m_ref[r, h], stat)
            stat = jnp.where(lane == HD // 2 + h, l_ref[r, h], stat)
        stat_out[r] = stat


def finish_kernel(n_seq, n_tp, group, q, kg, mask, part, stat, weight, out,
                  got, gstat, wbuf, att, tree, pbuf, prbuf,
                  asem, arsem, tsem, trsem, wsem, psem, prsem, lsem):
    me = lax.axis_index("seq")
    tp = lax.axis_index("tp")
    rows, width = q.shape
    heads = width // HD
    out_w = out.shape[1]
    barrier = pltpu.get_barrier_semaphore()
    for d in range(1, n_seq):
        pl.semaphore_signal(barrier, inc=1, device_id={"seq": lax.rem(me + d, n_seq)},
                            device_id_type=MESH)
    for d in range(1, n_tp):
        pl.semaphore_signal(barrier, inc=1, device_id={"tp": lax.rem(tp + d, n_tp)},
                            device_id_type=MESH)
    own_part = pltpu.make_async_copy(part.at[me], got.at[me], lsem.at[0])
    own_stat = pltpu.make_async_copy(stat.at[me], gstat.at[me], lsem.at[1])
    own_part.start()
    own_stat.start()
    loads = []
    for t in range(n_tp):
        c = pltpu.make_async_copy(weight.at[:, pl.ds(t * out_w, out_w)], wbuf.at[t], wsem.at[t])
        c.start()
        loads.append(c)
    pl.semaphore_wait(barrier, n_seq + n_tp - 2)
    sent = []
    for d in range(1, n_seq):
        peer = lax.rem(me + d, n_seq)
        for src, dst, s, r in ((stat, gstat, tsem, trsem), (part, got, asem, arsem)):
            c = pltpu.make_async_remote_copy(
                src_ref=src.at[peer], dst_ref=dst.at[me], send_sem=s.at[d - 1],
                recv_sem=r.at[me], device_id={"seq": peer}, device_id_type=MESH)
            c.start()
            sent.append(c)

    scale = 1.0 / math.sqrt(HD)
    allowed = mask[me] == 1
    tree_m = []
    tree_l = []
    for h in range(heads):
        cols = slice(h * HD, (h + 1) * HD)
        keys = jnp.concatenate([kg[g, 0, :, cols] for g in range(group)], axis=0)
        values = jnp.concatenate([kg[g, 1, :, cols] for g in range(group)], axis=0)
        x = lax.dot_general(q[:, cols], keys, NT, preferred_element_type=jnp.float32) * scale
        x = jnp.where(allowed, x, NEGATIVE)
        top = jnp.max(x, axis=1, keepdims=True)
        p = jnp.where(allowed, jnp.exp(x - top), 0.0)
        tree_m.append(top)
        tree_l.append(jnp.sum(p, axis=1, keepdims=True))
        tree[:, cols] = jnp.dot(p.astype(jnp.bfloat16), values, preferred_element_type=jnp.float32)

    own_part.wait()
    own_stat.wait()
    for d in range(1, n_seq):
        src = lax.rem(me + n_seq - d, n_seq)
        for a, b, s, r in ((stat, gstat, tsem, trsem), (part, got, asem, arsem)):
            pltpu.make_async_remote_copy(
                src_ref=a.at[src], dst_ref=b.at[src], send_sem=s.at[d - 1],
                recv_sem=r.at[src], device_id={"seq": src}, device_id_type=MESH).wait_recv()
    for h in range(heads):
        cols = slice(h * HD, (h + 1) * HD)
        top = tree_m[h]
        for i in range(n_seq):
            top = jnp.maximum(top, gstat[i, :, h:h + 1])
        f = jnp.exp(tree_m[h] - top)
        den = f * tree_l[h]
        num = f * tree[:, cols]
        for i in range(n_seq):
            f = jnp.exp(gstat[i, :, h:h + 1] - top)
            den = den + f * gstat[i, :, HD // 2 + h:HD // 2 + h + 1]
            num = num + f * got[i, :, cols].astype(jnp.float32)
        att[:, cols] = (num / den).astype(jnp.bfloat16)
    for c in loads:
        c.wait()
    for d in range(1, n_tp):
        peer = lax.rem(tp + d, n_tp)
        pbuf[d - 1] = jnp.dot(att[...], wbuf[peer],
                              preferred_element_type=jnp.float32).astype(jnp.bfloat16)
        c = pltpu.make_async_remote_copy(
            src_ref=pbuf.at[d - 1], dst_ref=prbuf.at[d - 1], send_sem=psem.at[d - 1],
            recv_sem=prsem.at[d - 1], device_id={"tp": peer}, device_id_type=MESH)
        c.start()
        sent.append(c)
    total = jnp.dot(att[...], wbuf[tp], preferred_element_type=jnp.float32)
    for d in range(1, n_tp):
        pltpu.make_async_remote_copy(
            src_ref=pbuf.at[d - 1], dst_ref=prbuf.at[d - 1], send_sem=psem.at[d - 1],
            recv_sem=prsem.at[d - 1], device_id={"tp": lax.rem(tp + d, n_tp)},
            device_id_type=MESH).wait_recv()
        total = total + prbuf[d - 1].astype(jnp.float32)
    out[...] = total.astype(out.dtype)
    for c in sent:
        c.wait_send()


def body(draft_q, draft_kv, kv_pool, page_table, cache_len, tree_mask, accepted_rows, out_weight):
    n_seq = lax.axis_size("seq")
    n_tp = lax.axis_size("tp")
    rows, width = draft_q.shape
    heads = width // HD
    n_req, n_pages = page_table.shape
    n_draft = tree_mask.shape[1]
    n_slots, page_len = kv_pool.shape[1:3]
    group = n_seq // n_req
    out_w = out_weight.shape[1] // n_tp
    bf16, f32 = jnp.bfloat16, jnp.float32
    dma = pltpu.SemaphoreType.DMA

    query_all, group_kv = pl.pallas_call(
        functools.partial(gather_kernel, n_req, group),
        out_shape=(jax.ShapeDtypeStruct((n_seq, rows, width), bf16),
                   jax.ShapeDtypeStruct((group, 2, rows, width), bf16)),
        in_specs=[ANY, ANY],
        out_specs=(ANY, ANY),
        scratch_shapes=[dma((n_req + group - 2,)), dma((n_seq,)),
                        dma(((n_req - 1) * (group - 1),)), dma((group - 1,)), dma((group,)),
                        dma((2,))],
        compiler_params=pltpu.CompilerParams(collective_id=0, has_side_effects=True),
    )(draft_q, draft_kv)

    first = (lax.axis_index("seq") * n_slots).astype(jnp.int32).reshape(1)
    part, stat = pl.pallas_call(
        page_kernel,
        out_shape=(jax.ShapeDtypeStruct((n_req, n_draft, width), bf16),
                   jax.ShapeDtypeStruct((n_req, n_draft, HD), f32)),
        in_specs=[SMEM, SMEM, SMEM, VMEM, ANY],
        out_specs=(VMEM, VMEM),
        scratch_shapes=[pltpu.VMEM((n_slots, page_len, width), bf16),
                        pltpu.VMEM((n_slots, page_len, width), bf16),
                        pltpu.VMEM((n_req, heads, n_draft, HD), f32),
                        pltpu.VMEM((n_req, heads, n_draft, HD), f32),
                        pltpu.VMEM((n_req, n_draft, width), f32),
                        pltpu.SMEM((n_slots,), jnp.int32),
                        pltpu.SMEM((n_slots,), jnp.int32),
                        dma((n_slots,)), dma((n_slots,))],
        compiler_params=pltpu.CompilerParams(vmem_limit_bytes=32 << 20),
        cost_estimate=pl.CostEstimate(flops=10 ** 10, bytes_accessed=3 * 10 ** 7,
                                      transcendentals=10 ** 6),
    )(page_table, cache_len, first, query_all.reshape(n_req, n_draft, width), kv_pool)

    layer_out = pl.pallas_call(
        functools.partial(finish_kernel, n_seq, n_tp, group),
        out_shape=jax.ShapeDtypeStruct((rows, out_w), bf16),
        in_specs=[VMEM, VMEM, VMEM, ANY, ANY, ANY],
        out_specs=VMEM,
        scratch_shapes=[pltpu.VMEM((n_seq, rows, width), bf16),
                        pltpu.VMEM((n_seq, rows, HD), f32),
                        pltpu.VMEM((n_tp, width, out_w), bf16),
                        pltpu.VMEM((rows, width), bf16),
                        pltpu.VMEM((rows, width), f32),
                        pltpu.VMEM((n_tp - 1, rows, out_w), bf16),
                        pltpu.VMEM((n_tp - 1, rows, out_w), bf16),
                        dma((n_seq - 1,)), dma((n_seq,)), dma((n_seq - 1,)), dma((n_seq,)),
                        dma((n_tp,)), dma((n_tp - 1,)), dma((n_tp - 1,)), dma((2,))],
        compiler_params=pltpu.CompilerParams(collective_id=1, has_side_effects=True,
                                             vmem_limit_bytes=32 << 20),
        cost_estimate=pl.CostEstimate(flops=10 ** 10, bytes_accessed=3 * 10 ** 7,
                                      transcendentals=10 ** 6),
    )(draft_q, group_kv, tree_mask.reshape(n_seq, rows, n_draft),
      part.reshape(n_seq, rows, width), stat.reshape(n_seq, rows, HD), out_weight)

    kv_all = lax.all_gather(draft_kv, "seq", axis=1, tiled=True)
    picked = jnp.concatenate(
        [accepted_rows, jnp.full((n_req, page_len - n_draft), -1, jnp.int32)], axis=1)
    onehot = (picked[:, :, None] == jnp.arange(n_draft, dtype=jnp.int32)[None, None, :]).astype(bf16)
    accepted_kv = jnp.einsum(
        "rji,crid->crjd", onehot, kv_all.reshape(2, n_req, n_draft, width),
        preferred_element_type=f32).astype(bf16)
    return (layer_out, accepted_kv)


def solution(mesh):
    return jax.shard_map(
        body,
        mesh=mesh,
        in_specs=(P("seq", "tp"), P(None, "seq", "tp"), P(None, "seq", None, "tp"),
                  P(), P(), P(), P(), P("tp", None)),
        out_specs=(P("seq", "tp"), P(None, None, None, "tp")),
        check_vma=False,
    )
```

time: 173 us -> 78.9 us (0.46); the launches traced: 171 us -> 78.6 us
  Pallas kernels: 0 us -> 53.8 us
  waiting for transfers between devices: 40.6 us -> 0.7 us
  local copies, waits for them, and re-layouts: 38.9 us -> 7.94 us
  matrix products: 25.5 us -> 1.98 us
  blocking collectives: 23.3 us -> 0 us
  starting transfers between devices: 18.8 us -> 0.04 us
  other arithmetic: 9.36 us -> 0 us
    pallas_call x0 -> x3, Pallas kernels: none -> 53.8 us  [the longest x1 32.3 us: body(): pl.pallas_call(functools.partial(finish_kernel, n_seq, n_tp, group), out_...]
    dot_general x8 -> x1, matrix products: 25.5 us -> 1.98 us  [body(): jnp.einsum('rji,crid->crjd', onehot, kv_all.reshape(2, n_req, n_draft, wi...]
    all_gather x1 -> x0, blocking collectives: 23.3 us -> none  [body(): lax.all_gather(draft_q, 'seq', axis=0, tiled=True)]
    reduce_scatter x1 -> x0, waiting for transfers between devices: 21.5 us -> none  [body(): lax.psum_scatter(partial_value, 'tp', scatter_dimension=1, tiled=True)]
    all_gather x1, waiting for transfers between devices: 19.1 us -> 0.02 us  [body(): kv_all = lax.all_gather(draft_kv, 'seq', axis=1, tiled=True)]
    all_to_all x3 -> x0, starting transfers between devices: 18.8 us -> none  [the longest x1 7.96 us: body(): lax.all_to_all(local_total, 'seq', split_axis=0, concat_axis=0, tiled=True)]
    unnamed x21 -> x20, local copies, waits for them, and re-layouts: 24 us -> 7.94 us
    slice x2 -> x0, local copies, waits for them, and re-layouts: 10.1 us -> none  [the longest x1 6.01 us: body(): page_keys = kv_pool[0].reshape(n_slots, page_len, heads_loc, HD)]
  transfers between devices with their start and end apart: 5 -> 1, of which waited for: 2 -> 0; matrix products, arithmetic and copies ran while one was open for 22% -> 0% of each run, Pallas kernels for 0% -> 68%
where the time goes in v1:
time: 78.9 us; the launch traced here: 78.6 us
  Pallas kernels  53.8 us (68%)
  between operations  14.1 us (18%)
  local copies, waits for them, and re-layouts  7.94 us (10%)
  matrix products  1.98 us (3%)
    pallas_call x1, Pallas kernels, body(): pl.pallas_call(functools.partial(finish_kernel, n_seq, n_tp, group), out_...  32.3 us
    pallas_call x1, Pallas kernels, body(): pl.pallas_call(functools.partial(gather_kernel, n_req, group), out_shape=...  12 us
    pallas_call x1, Pallas kernels, body(): pl.pallas_call(page_kernel, out_shape=(jax.ShapeDtypeStruct((n_req, n_dra...  9.41 us
    unnamed x20, local copies, waits for them, and re-layouts  7.94 us
    dot_general x1, matrix products, body(): jnp.einsum('rji,crid->crjd', onehot, kv_all.reshape(2, n_req, n_draft, wi...  1.98 us
  transfers between devices with their start and end apart: 1, of which 0 were waited for; matrix products, arithmetic and copies ran while one was open for 0% of the time, Pallas kernels for 68%

profile of v1, /device:TPU:11, one launch (start us, length us, event | category | flops | bytes accessed | tf_op | source)
XLA Modules:
  0.0 78.6 jit_solution(10287361133833728987)
XLA Ops:
  7.2 0.0 all-gather.2.cloned.1.call-start
  7.2 0.7 all-gather.2.cloned.1.call-update
  7.9 12.0 %shard_map.95 = (bf16[8,32,1024]{2,1,0:T(8,128)(2,1)}, bf16[2,2,32,1024]{3,2,1,0:T(8,128)(2,1)}) custom-call(bf16[32,1024]{1,0:T(8,128)(2,1)} %q.3, bf16[2,32,1024]{2,1,0:T(8,128)(2,1)} %kv.1), custom_call_target="tpu_custom_call" | custom-call | tf_op jit(solution)/shard_map/pallas_call | solution.py:265
  20.0 0.0 copy-start.1
  20.0 3.4 %copy-done.1 = bf16[2,16,128,1024]{3,2,1,0:T(8,128)(2,1)S(1)} copy-done((bf16[2,16,128,1024]{3,2,1,0:T(8,128)(2,1)S(1)}, bf16[2,16,128,1024]{3,2,1,0:T(8,128)(2,1)}, u32[]{:S(2)}) %copy-start.1) | copy-done | bytes 8388632
  23.4 0.0 copy-start.3
  23.4 1.0 %copy-done.3 = bf16[8,32,1024]{2,1,0:T(8,128)(2,1)S(1)} copy-done((bf16[8,32,1024]{2,1,0:T(8,128)(2,1)S(1)}, bf16[8,32,1024]{2,1,0:T(8,128)(2,1)}, u32[]{:S(2)}) %copy-start.3) | copy-done | bytes 524312
  24.4 0.0 copy-start.6
  24.4 0.7 copy-done.6
  25.1 0.0 copy-start.7
  25.1 0.7 copy-done.7
  25.8 0.0 copy-start
  25.8 0.0 copy-start.2
  25.8 0.0 copy-start.4
  25.8 0.0 copy-start.5
  25.8 9.4 %shard_map.96 = (bf16[4,64,1024]{2,1,0:T(8,128)(2,1)S(1)}, f32[4,64,128]{2,1,0:T(8,128)S(1)}) custom-call(s32[4,32]{1,0:T(4,128)S(1)} %copy-done.6, s32[4]{0:T(128)S(1)} %copy-done.7, s32[1]{0:T(128)} %bitcast.1.first, bf16[4,64,1024]{2,1,0:T(8,128)(2,1)S(1)} %bitcast.13, bf16[2,16,128,1024]{3,2,1,0:T(8,128)(2,1)S(1)} %copy-done.1), custom_call_target="tpu_custom_call" | custom-call | flops 10000000000 | bytes 30000000 | tf_op jit(solution)/shard_map/pallas_call | solution.py:278
  35.2 0.0 copy-done
  35.2 0.0 copy-done.2
  35.2 0.0 copy-done.4
  35.2 0.0 copy-done.5
  35.2 0.0 copy-start.8
  35.2 32.3 %shard_map.97 = bf16[32,1024]{1,0:T(8,128)(2,1)S(1)} custom-call(bf16[32,1024]{1,0:T(8,128)(2,1)S(1)} %copy-done, bf16[2,2,32,1024]{3,2,1,0:T(8,128)(2,1)S(1)} %copy-done.4, s32[8,32,64]{2,1,0:T(8,128)S(1)} %bitcast.14, bf16[8,32,1024]{2,1,0:T(8,128)(2,1)S(1)} %bitcast.15, f32[8,32,128]{2,1,0:T(8,128)S(1)} %bitcast.16, bf16[1024,4096]{1,0:T(8,128)(2,1)S(1)} %copy-done.2), custom_call_target="tpu_custom_call" | custom-call | flops 10000000000 | bytes 30000000 | tf_op jit(solution)/shard_map/pallas_call | solution.py:297
  67.6 0.0 copy-done.8
  67.6 0.0 all-gather.2.cloned.1.call-done
  67.6 2.0 %convert_bitcast_fusion = bf16[2,4,128,1024]{3,2,0,1:T(8,128)(2,1)S(1)} fusion(bf16[2,4,64,1024]{3,2,1,0:T(8,128)(2,1)} %bitcast.17, s32[4,128]{1,0:T(4,128)S(1)} %concatenate.3), kind=kOutput, calls=%fused_computation | convolution fusion | flops 135299072 | bytes 3147776 | tf_op jit(solution)/shard_map/rji,crid->crjd/dot_general | solution.py:322
  69.6 1.5 %copy.12 = bf16[2,4,128,1024]{3,2,1,0:T(8,128)(2,1)} copy(bf16[2,4,128,1024]{3,2,0,1:T(8,128)(2,1)S(1)} %convert_bitcast_fusion) | data formatting | bytes 4194304
  71.1 0.6 copy.17
  (1 shorter events, 0.0 us)
Async XLA Ops:
  7.2 60.5 %all-gather.2.cloned.1.call-start = ((), (), s32[]{:S(2)}) async-start(), calls=%async_computation | async-start | bytes 1179648 | tf_op jit(solution)/shard_map/all_gather | solution.py:318
  20.0 3.4 %copy-start.1 = (bf16[2,16,128,1024]{3,2,1,0:T(8,128)(2,1)S(1)}, bf16[2,16,128,1024]{3,2,1,0:T(8,128)(2,1)}, u32[]{:S(2)}) copy-start(bf16[2,16,128,1024]{3,2,1,0:T(8,128)(2,1)} %pool.1) | copy-start | bytes 25165828
  23.4 1.0 %copy-start.3 = (bf16[8,32,1024]{2,1,0:T(8,128)(2,1)S(1)}, bf16[8,32,1024]{2,1,0:T(8,128)(2,1)}, u32[]{:S(2)}) copy-start(bf16[8,32,1024]{2,1,0:T(8,128)(2,1)} %get-tuple-element.7) | copy-start | bytes 1572868
  24.4 0.7 copy-start.6
  25.1 0.7 copy-start.7
  25.8 9.4 %copy-start = (bf16[32,1024]{1,0:T(8,128)(2,1)S(1)}, bf16[32,1024]{1,0:T(8,128)(2,1)}, u32[]{:S(2)}) copy-start(bf16[32,1024]{1,0:T(8,128)(2,1)} %q.3) | copy-start | bytes 196612
  25.8 9.4 %copy-start.2 = (bf16[1024,4096]{1,0:T(8,128)(2,1)S(1)}, bf16[1024,4096]{1,0:T(8,128)(2,1)}, u32[]{:S(2)}) copy-start(bf16[1024,4096]{1,0:T(8,128)(2,1)} %weight.1) | copy-start | bytes 25165828
  25.8 9.4 %copy-start.4 = (bf16[2,2,32,1024]{3,2,1,0:T(8,128)(2,1)S(1)}, bf16[2,2,32,1024]{3,2,1,0:T(8,128)(2,1)}, u32[]{:S(2)}) copy-start(bf16[2,2,32,1024]{3,2,1,0:T(8,128)(2,1)} %get-tuple-element.6.kg) | copy-start | bytes 786436
  25.8 9.5 %copy-start.5 = (s32[4,64,64]{2,1,0:T(8,128)S(1)}, s32[4,64,64]{2,1,0:T(8,128)}, u32[]{:S(2)}) copy-start(s32[4,64,64]{2,1,0:T(8,128)} %param.13) | copy-start | bytes 196612
  35.2 32.4 %copy-start.8 = (s32[4,64]{1,0:T(4,128)S(1)}, s32[4,64]{1,0:T(4,128)}, u32[]{:S(2)}) copy-start(s32[4,64]{1,0:T(4,128)} %param.14) | copy-start | bytes 3076
Sparse Core Ops, SparseCore 0:
  10.2 46.8 all-gather.1

commit v2 on v1

v2 whole, which is shorter than its diff:
```python
import functools
import math

import jax
import jax.numpy as jnp
from jax import lax
from jax.experimental import pallas as pl
from jax.experimental.pallas import tpu as pltpu
from jax.sharding import PartitionSpec as P

HD = 128
NEGATIVE = -1e30
MESH = pl.DeviceIdType.MESH
ANY = pl.BlockSpec(memory_space=pl.ANY)
VMEM = pl.BlockSpec(memory_space=pltpu.VMEM)
SMEM = pl.BlockSpec(memory_space=pltpu.SMEM)
NT = (((1,), (1,)), ((), ()))


def fused_kernel(n_req, n_pages, n_seq, n_tp, group, code, cache_len, mask, q, kv, pool, weight,
                 out, kva,
                 qa, kbuf, vbuf, m_st, l_st, acc_st, part, stat, got, gstat, kg, wbuf, att, tree,
                 pbuf, prbuf, last,
                 qsem, qrsem, fsem, cssem, crsem, cfsem, lsem, ksem, vsem, gsem,
                 asem, arsem, tsem, trsem, wsem, psem, prsem):
    me = lax.axis_index("seq")
    tp = lax.axis_index("tp")
    grp = me // group
    inner = lax.rem(me, group)
    n_slots, page_len, width = kbuf.shape
    rows = qa.shape[1] // group
    n_draft = qa.shape[1]
    heads = width // HD
    out_w = out.shape[1]
    scale = 1.0 / math.sqrt(HD)

    def across(d):
        return lax.rem(grp + d, n_req) * group + inner

    def other(d):
        return grp * group + lax.rem(inner + d, group)

    def remote(a, b, s, r, where):
        return pltpu.make_async_remote_copy(
            src_ref=a, dst_ref=b, send_sem=s, recv_sem=r, device_id=where, device_id_type=MESH)

    def block(i):
        return qa.at[i // group, pl.ds(pl.multiple_of(lax.rem(i, group) * rows, rows), rows)]

    barrier = pltpu.get_barrier_semaphore()
    for d in range(1, n_seq):
        pl.semaphore_signal(barrier, inc=1, device_id={"seq": lax.rem(me + d, n_seq)},
                            device_id_type=MESH)
    for d in range(1, n_tp):
        pl.semaphore_signal(barrier, inc=1, device_id={"tp": lax.rem(tp + d, n_tp)},
                            device_id_type=MESH)
    own_q = pltpu.make_async_copy(q, block(me), lsem.at[0])
    own_q.start()
    own_kv = pltpu.make_async_copy(kv, kva.at[me], lsem.at[1])
    own_kv.start()
    for s in range(n_slots):
        pltpu.make_async_copy(pool.at[0, s], kbuf.at[s], ksem.at[s]).start()
        pltpu.make_async_copy(pool.at[1, s], vbuf.at[s], vsem.at[s]).start()
    loads = []
    for t in range(n_tp):
        c = pltpu.make_async_copy(weight.at[:, pl.ds(t * out_w, out_w)], wbuf.at[t], wsem.at[t])
        c.start()
        loads.append(c)
    m_st[0] = jnp.full(m_st.shape[1:], NEGATIVE, jnp.float32)
    l_st[0] = jnp.zeros(l_st.shape[1:], jnp.float32)
    acc_st[0] = jnp.zeros(acc_st.shape[1:], jnp.float32)
    for r in range(n_req):
        last[r] = 0
    pl.semaphore_wait(barrier, n_seq + n_tp - 2)

    sent = []

    def send(*args):
        c = remote(*args)
        c.start()
        sent.append(c)

    for d in range(n_req - 1, 0, -1):
        send(q, block(me), qsem.at[d - 1], qrsem.at[me], {"seq": across(d)})
    for d in range(1, group):
        send(q, block(me), qsem.at[n_req - 2 + d], qrsem.at[me], {"seq": other(d)})
    for d in range(1, group):
        send(kv, kva.at[me], cssem.at[n_req - 2 + d], crsem.at[me], {"seq": other(d)})
    for d in range(n_req - 1, 0, -1):
        send(kv, kva.at[me], cssem.at[d - 1], crsem.at[me], {"seq": across(d)})

    def q_arrived(b):
        remote(q, block(b), qsem.at[0], qrsem.at[b], {"seq": other(1)}).wait_recv()

    def kv_arrived(b):
        remote(kv, kva.at[b], cssem.at[0], crsem.at[b], {"seq": other(1)}).wait_recv()

    for e in range(1, n_req):
        b = across(e)
        q_arrived(b)
        for d in range(1, group):
            send(block(b), block(b), fsem.at[(e - 1) * (group - 1) + d - 1], qrsem.at[b],
                 {"seq": other(d)})
    for d in range(1, group):
        q_arrived(other(d))
        for e in range(1, n_req):
            q_arrived(lax.rem(grp + e, n_req) * group + lax.rem(inner + d, group))
    own_q.wait()

    def forward(e, d, start):
        b = across(e)
        c = remote(kva.at[b], kva.at[b], cfsem.at[(e - 1) * (group - 1) + d - 1], crsem.at[b],
                   {"seq": other(d)})
        if start:
            c.start()
        else:
            c.wait_send()

    def step(s, carry):
        pltpu.make_async_copy(pool.at[0, s], kbuf.at[s], ksem.at[s]).wait()
        pltpu.make_async_copy(pool.at[1, s], vbuf.at[s], vsem.at[s]).wait()
        number = code[s]
        place = jnp.maximum(number - 1, 0)
        r = lax.div(place, n_pages)
        left = jnp.where(number > 0, cache_len[r] - (place - r * n_pages) * page_len, 0)
        prev = last[r]
        scores = []
        for h in range(heads):
            cols = slice(h * HD, (h + 1) * HD)
            scores.append(lax.dot_general(
                qa[r, :, cols], kbuf[s, :, cols], NT, preferred_element_type=jnp.float32))
        live = lax.broadcasted_iota(jnp.int32, scores[0].shape, 1) < left
        probs = []
        scales = []
        for h in range(heads):
            x = jnp.where(live, scores[h] * scale, NEGATIVE)
            old = m_st[prev, h]
            new = jnp.maximum(old, jnp.max(x, axis=1, keepdims=True))
            p = jnp.exp(x - new)
            a = jnp.exp(old - new)
            m_st[s + 1, h] = new
            l_st[s + 1, h] = a * l_st[prev, h] + jnp.sum(p, axis=1, keepdims=True)
            probs.append(p.astype(jnp.bfloat16))
            scales.append(a)
        for h in range(heads):
            cols = slice(h * HD, (h + 1) * HD)
            o = jnp.dot(probs[h], vbuf[s, :, cols], preferred_element_type=jnp.float32)
            acc_st[s + 1, :, cols] = scales[h] * acc_st[prev, :, cols] + o
        for i in range(n_req):
            last[i] = jnp.where((left > 0) & (r == i), s + 1, last[i])
        return carry

    cuts = [n_slots * e // n_req for e in range(n_req + 1)]
    for e in range(n_req):
        lax.fori_loop(cuts[e], cuts[e + 1], step, 0)
        if e + 1 < n_req:
            kv_arrived(across(e + 1))
            for d in range(1, group):
                forward(e + 1, d, True)

    lane = lax.broadcasted_iota(jnp.int32, (n_draft, HD), 1)
    for r in range(n_req):
        at = last[r]
        acc = acc_st[at].astype(jnp.bfloat16)
        info = jnp.zeros((n_draft, HD), jnp.float32)
        for h in range(heads):
            info = jnp.where(lane == h, m_st[at, h], info)
            info = jnp.where(lane == HD // 2 + h, l_st[at, h], info)
        for g in range(group):
            part[r * group + g] = acc[g * rows:(g + 1) * rows]
            stat[r * group + g] = info[g * rows:(g + 1) * rows]
    own_part = pltpu.make_async_copy(part.at[me], got.at[me], lsem.at[2])
    own_stat = pltpu.make_async_copy(stat.at[me], gstat.at[me], lsem.at[3])
    own_part.start()
    own_stat.start()
    for d in range(1, n_seq):
        peer = lax.rem(me + d, n_seq)
        send(stat.at[peer], gstat.at[me], tsem.at[d - 1], trsem.at[me], {"seq": peer})
        send(part.at[peer], got.at[me], asem.at[d - 1], arsem.at[me], {"seq": peer})

    own_kv.wait()
    for d in range(1, group):
        kv_arrived(other(d))
    tree_in = []
    for g in range(group):
        c = pltpu.make_async_copy(kva.at[grp * group + g], kg.at[g], gsem.at[g])
        c.start()
        tree_in.append(c)
    for c in tree_in:
        c.wait()
    allowed = mask[me] == 1
    mine = qa[grp, pl.ds(pl.multiple_of(inner * rows, rows), rows), :]
    tree_m = []
    tree_l = []
    for h in range(heads):
        cols = slice(h * HD, (h + 1) * HD)
        keys = jnp.concatenate([kg[g, 0, :, cols] for g in range(group)], axis=0)
        values = jnp.concatenate([kg[g, 1, :, cols] for g in range(group)], axis=0)
        x = lax.dot_general(mine[:, cols], keys, NT, preferred_element_type=jnp.float32) * scale
        x = jnp.where(allowed, x, NEGATIVE)
        top = jnp.max(x, axis=1, keepdims=True)
        p = jnp.where(allowed, jnp.exp(x - top), 0.0)
        tree_m.append(top)
        tree_l.append(jnp.sum(p, axis=1, keepdims=True))
        tree[:, cols] = jnp.dot(p.astype(jnp.bfloat16), values, preferred_element_type=jnp.float32)

    own_part.wait()
    own_stat.wait()
    for d in range(1, n_seq):
        i = lax.rem(me + n_seq - d, n_seq)
        remote(stat.at[i], gstat.at[i], tsem.at[d - 1], trsem.at[i], {"seq": i}).wait_recv()
        remote(part.at[i], got.at[i], asem.at[d - 1], arsem.at[i], {"seq": i}).wait_recv()
    for h in range(heads):
        cols = slice(h * HD, (h + 1) * HD)
        top = tree_m[h]
        for i in range(n_seq):
            top = jnp.maximum(top, gstat[i, :, h:h + 1])
        f = jnp.exp(tree_m[h] - top)
        den = f * tree_l[h]
        num = f * tree[:, cols]
        for i in range(n_seq):
            f = jnp.exp(gstat[i, :, h:h + 1] - top)
            den = den + f * gstat[i, :, HD // 2 + h:HD // 2 + h + 1]
            num = num + f * got[i, :, cols].astype(jnp.float32)
        att[:, cols] = (num / den).astype(jnp.bfloat16)
    for c in loads:
        c.wait()
    for d in range(1, n_tp):
        peer = lax.rem(tp + d, n_tp)
        pbuf[d - 1] = jnp.dot(att[...], wbuf[peer],
                              preferred_element_type=jnp.float32).astype(jnp.bfloat16)
        c = pltpu.make_async_remote_copy(
            src_ref=pbuf.at[d - 1], dst_ref=prbuf.at[d - 1], send_sem=psem.at[d - 1],
            recv_sem=prsem.at[d - 1], device_id={"tp": peer}, device_id_type=MESH)
        c.start()
        sent.append(c)
    total = jnp.dot(att[...], wbuf[tp], preferred_element_type=jnp.float32)
    for d in range(1, n_tp):
        pltpu.make_async_remote_copy(
            src_ref=pbuf.at[d - 1], dst_ref=prbuf.at[d - 1], send_sem=psem.at[d - 1],
            recv_sem=prsem.at[d - 1], device_id={"tp": lax.rem(tp + d, n_tp)},
            device_id_type=MESH).wait_recv()
        total = total + prbuf[d - 1].astype(jnp.float32)
    out[...] = total.astype(out.dtype)
    for d in range(1, group):
        for e in range(1, n_req):
            kv_arrived(lax.rem(grp + e, n_req) * group + lax.rem(inner + d, group))
    for e in range(1, n_req):
        for d in range(1, group):
            forward(e, d, False)
    for c in sent:
        c.wait_send()


def accept_kernel(rows_ref, kv, out):
    group, rows, width = kv.shape[1], kv.shape[3], kv.shape[4]
    n_draft = group * rows
    pick = lax.broadcasted_iota(jnp.int32, (n_draft, n_draft), 0) == rows_ref[0]
    blocks = jnp.concatenate([kv[0, g, 0] for g in range(group)], axis=0)
    out[0, 0, :n_draft] = lax.dot_general(
        pick.astype(jnp.bfloat16), blocks, (((0,), (0,)), ((), ())),
        preferred_element_type=jnp.float32).astype(out.dtype)
    out[0, 0, n_draft:] = jnp.zeros((out.shape[2] - n_draft, width), out.dtype)


def body(draft_q, draft_kv, kv_pool, page_table, cache_len, tree_mask, accepted_rows, out_weight):
    n_seq = lax.axis_size("seq")
    n_tp = lax.axis_size("tp")
    rows, width = draft_q.shape
    heads = width // HD
    n_req, n_pages = page_table.shape
    n_draft = tree_mask.shape[1]
    n_slots, page_len = kv_pool.shape[1:3]
    group = n_seq // n_req
    out_w = out_weight.shape[1] // n_tp
    bf16, f32 = jnp.bfloat16, jnp.float32
    dma = pltpu.SemaphoreType.DMA

    slots = lax.axis_index("seq") * n_slots + jnp.arange(n_slots, dtype=jnp.int32)
    number = jnp.arange(1, n_req * n_pages + 1, dtype=jnp.int32)
    code = jnp.sum(jnp.where(page_table.reshape(1, -1) == slots[:, None], number[None], 0), axis=1)

    layer_out, kv_all = pl.pallas_call(
        functools.partial(fused_kernel, n_req, n_pages, n_seq, n_tp, group),
        out_shape=(jax.ShapeDtypeStruct((rows, out_w), bf16),
                   jax.ShapeDtypeStruct((n_seq, 2, rows, width), bf16)),
        in_specs=[SMEM, SMEM, VMEM, ANY, ANY, ANY, ANY],
        out_specs=(VMEM, ANY),
        scratch_shapes=[pltpu.VMEM((n_req, n_draft, width), bf16),
                        pltpu.VMEM((n_slots, page_len, width), bf16),
                        pltpu.VMEM((n_slots, page_len, width), bf16),
                        pltpu.VMEM((n_slots + 1, heads, n_draft, HD), f32),
                        pltpu.VMEM((n_slots + 1, heads, n_draft, HD), f32),
                        pltpu.VMEM((n_slots + 1, n_draft, width), f32),
                        pltpu.VMEM((n_seq, rows, width), bf16),
                        pltpu.VMEM((n_seq, rows, HD), f32),
                        pltpu.VMEM((n_seq, rows, width), bf16),
                        pltpu.VMEM((n_seq, rows, HD), f32),
                        pltpu.VMEM((group, 2, rows, width), bf16),
                        pltpu.VMEM((n_tp, width, out_w), bf16),
                        pltpu.VMEM((rows, width), bf16),
                        pltpu.VMEM((rows, width), f32),
                        pltpu.VMEM((n_tp - 1, rows, out_w), bf16),
                        pltpu.VMEM((n_tp - 1, rows, out_w), bf16),
                        pltpu.SMEM((n_req,), jnp.int32),
                        dma((n_req + group - 2,)), dma((n_seq,)),
                        dma(((n_req - 1) * (group - 1),)),
                        dma((n_req + group - 2,)), dma((n_seq,)),
                        dma(((n_req - 1) * (group - 1),)),
                        dma((4,)), dma((n_slots,)), dma((n_slots,)), dma((group,)),
                        dma((n_seq - 1,)), dma((n_seq,)), dma((n_seq - 1,)), dma((n_seq,)),
                        dma((n_tp,)), dma((n_tp - 1,)), dma((n_tp - 1,))],
        compiler_params=pltpu.CompilerParams(collective_id=0, has_side_effects=True,
                                             vmem_limit_bytes=58 << 20),
        cost_estimate=pl.CostEstimate(flops=10 ** 10, bytes_accessed=3 * 10 ** 7,
                                      transcendentals=10 ** 6),
    )(code, cache_len, tree_mask.reshape(n_seq, rows, n_draft), draft_q, draft_kv, kv_pool,
      out_weight)

    accepted_kv = pl.pallas_call(
        accept_kernel,
        grid=(n_req, 2),
        out_shape=jax.ShapeDtypeStruct((2, n_req, page_len, width), bf16),
        in_specs=[pl.BlockSpec((1, 1, n_draft), lambda r, c: (r, 0, 0)),
                  pl.BlockSpec((1, group, 1, rows, width), lambda r, c: (r, 0, c, 0, 0))],
        out_specs=pl.BlockSpec((1, 1, page_len, width), lambda r, c: (c, r, 0, 0)),
    )(accepted_rows.reshape(n_req, 1, n_draft), kv_all.reshape(n_req, group, 2, rows, width))
    return (layer_out, accepted_kv)


def solution(mesh):
    return jax.shard_map(
        body,
        mesh=mesh,
        in_specs=(P("seq", "tp"), P(None, "seq", "tp"), P(None, "seq", None, "tp"),
                  P(), P(), P(), P(), P("tp", None)),
        out_specs=(P("seq", "tp"), P(None, None, None, "tp")),
        check_vma=False,
    )
```

time: 78.9 us -> 59.1 us (0.75)
  between operations: 14.1 us -> 0.65 us
  local copies, waits for them, and re-layouts: 7.94 us -> 2.24 us
  matrix products: 1.98 us -> 0 us
  Pallas kernels: 53.8 us -> 54.9 us
    unnamed x20 -> x1, local copies, waits for them, and re-layouts: 7.94 us -> 1.47 us
    dot_general x1 -> x0, matrix products: 1.98 us -> none  [body(): jnp.einsum('rji,crid->crjd', onehot, kv_all.reshape(2, n_req, n_draft, wi...]
    pallas_call x3 -> x2, Pallas kernels: 53.8 us -> 54.9 us  [the longest x1 48.7 us: body(): pl.pallas_call(functools.partial(fused_kernel, n_req, n_pages, n_seq, n_t...]
  transfers between devices with their start and end apart: 1 -> 0, of which waited for: 0 -> 0; matrix products, arithmetic and copies ran while one was open for 0% -> 0% of each run, Pallas kernels for 68% -> 0%
where the time goes in v2:
time: 59.1 us; the launch traced here: 58.5 us
  Pallas kernels  54.9 us (93%)
  local copies, waits for them, and re-layouts  2.24 us (4%)
  other arithmetic  0.7 us (1%)
  between operations  0.65 us (1%)
    pallas_call x1, Pallas kernels, body(): pl.pallas_call(functools.partial(fused_kernel, n_req, n_pages, n_seq, n_t...  48.7 us
    pallas_call x1, Pallas kernels, body(): pl.pallas_call(accept_kernel, grid=(n_req, 2), out_shape=jax.ShapeDtypeSt...  6.2 us
    unnamed x1, local copies, waits for them, and re-layouts  1.47 us

profile of v2, /device:TPU:11, one launch (start us, length us, event | category | flops | bytes accessed | tf_op | source)
XLA Modules:
  0.0 58.5 jit_solution(6154617541399863482)
XLA Ops:
  0.6 0.8 %eq.15 = s32[128]{0:T(128)S(1)} reshape(s32[4,32]{1,0:T(4,128)} %param.11) | data formatting | bytes 1024 | tf_op jit(solution)/shard_map/eq | solution.py:281
  1.4 0.7 %select_reduce_fusion.code = s32[16]{0:T(128)} fusion(s32[128]{0:T(128)S(1)} %iota_add_fusion, s32[128]{0:T(128)S(1)} %eq.15, s32[16]{0:T(128)S(1)} %iota_add_fusion.1), kind=kLoop, calls=%fused_computation | loop fusion | flops 6128 | bytes 1152 | tf_op jit(solution)/shard_map/reduce_sum | solution.py:281
  2.1 48.7 %shard_map.95 = (bf16[32,1024]{1,0:T(8,128)(2,1)}, bf16[8,2,32,1024]{3,2,1,0:T(8,128)(2,1)}) custom-call(s32[16]{0:T(128)} %select_reduce_fusion.code, s32[4]{0:T(128)} %cache_len.1, s32[8,32,64]{2,1,0:T(8,128)} %bitcast.5, bf16[32,1024]{1,0:T(8,128)(2,1)} %q.1, bf16[2,32,1024]{2,1,0:T(8,128)(2,1)} %kv.1, bf16[2,16,128,1024]{3,2,1,0:T(8,128)(2,1)} %pool.1, ...), custom_call_target="tpu_custom_call" | custom-call | flops 10000000000 | bytes 30000000 | tf_op jit(solution)/shard_map/pallas_call | solution.py:283
  50.9 6.2 %shard_map.96 = bf16[2,4,128,1024]{3,2,1,0:T(8,128)(2,1)} custom-call(s32[4,1,64]{2,1,0:T(1,128)} %bitcast.4, bf16[4,2,2,32,1024]{4,3,2,1,0:T(8,128)(2,1)} %bitcast.3), custom_call_target="tpu_custom_call" | custom-call | tf_op jit(solution)/shard_map/pallas_call | solution.py:320
  57.1 1.5 %copy.11 = bf16[32,1024]{1,0:T(8,128)(2,1)} copy(bf16[32,1024]{1,0:T(8,128)(2,1)} %get-tuple-element.8) | data formatting | bytes 131072
  (2 shorter events, 0.0 us)

commit v3 on v2

--- a/solution.py
+++ b/solution.py
@@ -17,10 +17,10 @@
 NT = (((1,), (1,)), ((), ()))
 
 
-def fused_kernel(n_req, n_pages, n_seq, n_tp, group, code, cache_len, mask, q, kv, pool, weight,
+def fused_kernel(n_req, n_pages, n_seq, n_tp, group, table, cache_len, mask, q, kv, pool, weight,
                  out, kva,
                  qa, kbuf, vbuf, m_st, l_st, acc_st, part, stat, got, gstat, kg, wbuf, att, tree,
-                 pbuf, prbuf, last,
+                 pbuf, prbuf, last, code,
                  qsem, qrsem, fsem, cssem, crsem, cfsem, lsem, ksem, vsem, gsem,
                  asem, arsem, tsem, trsem, wsem, psem, prsem):
     me = lax.axis_index("seq")
@@ -58,6 +58,35 @@
     own_q.start()
     own_kv = pltpu.make_async_copy(kv, kva.at[me], lsem.at[1])
     own_kv.start()
+    m_st[0] = jnp.full(m_st.shape[1:], NEGATIVE, jnp.float32)
+    l_st[0] = jnp.zeros(l_st.shape[1:], jnp.float32)
+    acc_st[0] = jnp.zeros(acc_st.shape[1:], jnp.float32)
+    for r in range(n_req):
+        last[r] = 0
+    pl.semaphore_wait(barrier, n_seq + n_tp - 2)
+
+    sent = []
+
+    def send(*args):
+        c = remote(*args)
+        c.start()
+        sent.append(c)
+
+    for d in range(n_req - 1, 0, -1):
+        send(q, block(me), qsem.at[d - 1], qrsem.at[me], {"seq": across(d)})
+    for d in range(1, group):
+        send(q, block(me), qsem.at[n_req - 2 + d], qrsem.at[me], {"seq": other(d)})
+    for d in range(1, group):
+        send(kv, kva.at[me], cssem.at[n_req - 2 + d], crsem.at[me], {"seq": other(d)})
+    for d in range(n_req - 1, 0, -1):
+        send(kv, kva.at[me], cssem.at[d - 1], crsem.at[me], {"seq": across(d)})
+
+    def q_arrived(b):
+        remote(q, block(b), qsem.at[0], qrsem.at[b], {"seq": other(1)}).wait_recv()
+
+    def kv_arrived(b):
+        remote(kv, kva.at[b], cssem.at[0], crsem.at[b], {"seq": other(1)}).wait_recv()
+
     for s in range(n_slots):
         pltpu.make_async_copy(pool.at[0, s], kbuf.at[s], ksem.at[s]).start()
         pltpu.make_async_copy(pool.at[1, s], vbuf.at[s], vsem.at[s]).start()
@@ -66,34 +95,11 @@
         c = pltpu.make_async_copy(weight.at[:, pl.ds(t * out_w, out_w)], wbuf.at[t], wsem.at[t])
         c.start()
         loads.append(c)
-    m_st[0] = jnp.full(m_st.shape[1:], NEGATIVE, jnp.float32)
-    l_st[0] = jnp.zeros(l_st.shape[1:], jnp.float32)
-    acc_st[0] = jnp.zeros(acc_st.shape[1:], jnp.float32)
-    for r in range(n_req):
-        last[r] = 0
-    pl.semaphore_wait(barrier, n_seq + n_tp - 2)
-
-    sent = []
-
-    def send(*args):
-        c = remote(*args)
-        c.start()
-        sent.append(c)
-
-    for d in range(n_req - 1, 0, -1):
-        send(q, block(me), qsem.at[d - 1], qrsem.at[me], {"seq": across(d)})
-    for d in range(1, group):
-        send(q, block(me), qsem.at[n_req - 2 + d], qrsem.at[me], {"seq": other(d)})
-    for d in range(1, group):
-        send(kv, kva.at[me], cssem.at[n_req - 2 + d], crsem.at[me], {"seq": other(d)})
-    for d in range(n_req - 1, 0, -1):
-        send(kv, kva.at[me], cssem.at[d - 1], crsem.at[me], {"seq": across(d)})
-
-    def q_arrived(b):
-        remote(q, block(b), qsem.at[0], qrsem.at[b], {"seq": other(1)}).wait_recv()
-
-    def kv_arrived(b):
-        remote(kv, kva.at[b], cssem.at[0], crsem.at[b], {"seq": other(1)}).wait_recv()
+    shape = table.shape
+    number = (lax.broadcasted_iota(jnp.int32, shape, 0) * n_pages
+              + lax.broadcasted_iota(jnp.int32, shape, 1) + 1)
+    for s in range(n_slots):
+        code[s] = jnp.sum(jnp.where(table[...] == me * n_slots + s, number, 0))
 
     for e in range(1, n_req):
         b = across(e)
@@ -121,7 +127,7 @@
         pltpu.make_async_copy(pool.at[1, s], vbuf.at[s], vsem.at[s]).wait()
         number = code[s]
         place = jnp.maximum(number - 1, 0)
-        r = lax.div(place, n_pages)
+        r = jnp.minimum(lax.div(place, n_pages), n_req - 1)
         left = jnp.where(number > 0, cache_len[r] - (place - r * n_pages) * page_len, 0)
         prev = last[r]
         scores = []
@@ -150,13 +156,7 @@
             last[i] = jnp.where((left > 0) & (r == i), s + 1, last[i])
         return carry
 
-    cuts = [n_slots * e // n_req for e in range(n_req + 1)]
-    for e in range(n_req):
-        lax.fori_loop(cuts[e], cuts[e + 1], step, 0)
-        if e + 1 < n_req:
-            kv_arrived(across(e + 1))
-            for d in range(1, group):
-                forward(e + 1, d, True)
+    lax.fori_loop(0, n_slots, step, 0)
 
     lane = lax.broadcasted_iota(jnp.int32, (n_draft, HD), 1)
     for r in range(n_req):
@@ -177,6 +177,11 @@
         peer = lax.rem(me + d, n_seq)
         send(stat.at[peer], gstat.at[me], tsem.at[d - 1], trsem.at[me], {"seq": peer})
         send(part.at[peer], got.at[me], asem.at[d - 1], arsem.at[me], {"seq": peer})
+
+    for e in range(1, n_req):
+        kv_arrived(across(e))
+        for d in range(1, group):
+            forward(e, d, True)
 
     own_kv.wait()
     for d in range(1, group):
@@ -252,15 +257,38 @@
         c.wait_send()
 
 
-def accept_kernel(rows_ref, kv, out):
-    group, rows, width = kv.shape[1], kv.shape[3], kv.shape[4]
+def accept_kernel(rows_ref, kv, layer, out, layer_out, blocks, picked, zeros, isem, osem, zsem, lsem):
+    n_req, group, _, rows, width = kv.shape
     n_draft = group * rows
-    pick = lax.broadcasted_iota(jnp.int32, (n_draft, n_draft), 0) == rows_ref[0]
-    blocks = jnp.concatenate([kv[0, g, 0] for g in range(group)], axis=0)
-    out[0, 0, :n_draft] = lax.dot_general(
-        pick.astype(jnp.bfloat16), blocks, (((0,), (0,)), ((), ())),
-        preferred_element_type=jnp.float32).astype(out.dtype)
-    out[0, 0, n_draft:] = jnp.zeros((out.shape[2] - n_draft, width), out.dtype)
+    copies = []
+
+    def copy(a, b, sem):
+        c = pltpu.make_async_copy(a, b, sem)
+        c.start()
+        return c
+
+    loads = []
+    for r in range(n_req):
+        for c in range(2):
+            loads.append([copy(kv.at[r, g, c], blocks.at[r, c, pl.ds(g * rows, rows)],
+                               isem.at[r, c, g]) for g in range(group)])
+    copies.append(copy(layer, layer_out, lsem.at[0]))
+    zeros[...] = jnp.zeros(zeros.shape, zeros.dtype)
+    for r in range(n_req):
+        for c in range(2):
+            copies.append(copy(zeros, out.at[c, r, pl.ds(n_draft, zeros.shape[0])], zsem.at[r, c]))
+    for r in range(n_req):
+        pick = (lax.broadcasted_iota(jnp.int32, (n_draft, n_draft), 0)
+                == rows_ref[r:r + 1, :]).astype(jnp.bfloat16)
+        for c in range(2):
+            for load in loads[2 * r + c]:
+                load.wait()
+            picked[r, c] = lax.dot_general(
+                pick, blocks[r, c], (((0,), (0,)), ((), ())),
+                preferred_element_type=jnp.float32).astype(out.dtype)
+            copies.append(copy(picked.at[r, c], out.at[c, r, pl.ds(0, n_draft)], osem.at[r, c]))
+    for c in copies:
+        c.wait()
 
 
 def body(draft_q, draft_kv, kv_pool, page_table, cache_len, tree_mask, accepted_rows, out_weight):
@@ -276,15 +304,11 @@
     bf16, f32 = jnp.bfloat16, jnp.float32
     dma = pltpu.SemaphoreType.DMA
 
-    slots = lax.axis_index("seq") * n_slots + jnp.arange(n_slots, dtype=jnp.int32)
-    number = jnp.arange(1, n_req * n_pages + 1, dtype=jnp.int32)
-    code = jnp.sum(jnp.where(page_table.reshape(1, -1) == slots[:, None], number[None], 0), axis=1)
-
-    layer_out, kv_all = pl.pallas_call(
+    layer, kv_all = pl.pallas_call(
         functools.partial(fused_kernel, n_req, n_pages, n_seq, n_tp, group),
         out_shape=(jax.ShapeDtypeStruct((rows, out_w), bf16),
                    jax.ShapeDtypeStruct((n_seq, 2, rows, width), bf16)),
-        in_specs=[SMEM, SMEM, VMEM, ANY, ANY, ANY, ANY],
+        in_specs=[VMEM, SMEM, VMEM, ANY, ANY, ANY, ANY],
         out_specs=(VMEM, ANY),
         scratch_shapes=[pltpu.VMEM((n_req, n_draft, width), bf16),
                         pltpu.VMEM((n_slots, page_len, width), bf16),
@@ -302,7 +326,7 @@
                         pltpu.VMEM((rows, width), f32),
                         pltpu.VMEM((n_tp - 1, rows, out_w), bf16),
                         pltpu.VMEM((n_tp - 1, rows, out_w), bf16),
-                        pltpu.SMEM((n_req,), jnp.int32),
+                        pltpu.SMEM((n_req,), jnp.int32), pltpu.SMEM((n_slots,), jnp.int32),
                         dma((n_req + group - 2,)), dma((n_seq,)),
                         dma(((n_req - 1) * (group - 1),)),
                         dma((n_req + group - 2,)), dma((n_seq,)),
@@ -314,17 +338,21 @@
                                              vmem_limit_bytes=58 << 20),
         cost_estimate=pl.CostEstimate(flops=10 ** 10, bytes_accessed=3 * 10 ** 7,
                                       transcendentals=10 ** 6),
-    )(code, cache_len, tree_mask.reshape(n_seq, rows, n_draft), draft_q, draft_kv, kv_pool,
+    )(page_table, cache_len, tree_mask.reshape(n_seq, rows, n_draft), draft_q, draft_kv, kv_pool,
       out_weight)
 
-    accepted_kv = pl.pallas_call(
+    accepted_kv, layer_out = pl.pallas_call(
         accept_kernel,
-        grid=(n_req, 2),
-        out_shape=jax.ShapeDtypeStruct((2, n_req, page_len, width), bf16),
-        in_specs=[pl.BlockSpec((1, 1, n_draft), lambda r, c: (r, 0, 0)),
-                  pl.BlockSpec((1, group, 1, rows, width), lambda r, c: (r, 0, c, 0, 0))],
-        out_specs=pl.BlockSpec((1, 1, page_len, width), lambda r, c: (c, r, 0, 0)),
-    )(accepted_rows.reshape(n_req, 1, n_draft), kv_all.reshape(n_req, group, 2, rows, width))
+        out_shape=(jax.ShapeDtypeStruct((2, n_req, page_len, width), bf16),
+                   jax.ShapeDtypeStruct((rows, out_w), bf16)),
+        in_specs=[VMEM, ANY, ANY],
+        out_specs=(ANY, ANY),
+        scratch_shapes=[pltpu.VMEM((n_req, 2, n_draft, width), bf16),
+                        pltpu.VMEM((n_req, 2, n_draft, width), bf16),
+                        pltpu.VMEM((page_len - n_draft, width), bf16),
+                        dma((n_req, 2, group)), dma((n_req, 2)), dma((n_req, 2)), dma((1,))],
+        compiler_params=pltpu.CompilerParams(vmem_limit_bytes=58 << 20),
+    )(accepted_rows, kv_all.reshape(n_req, group, 2, rows, width), layer)
     return (layer_out, accepted_kv)
 
 

time: 59.1 us -> 51.8 us (0.88)
  Pallas kernels: 54.9 us -> 50.7 us
  local copies, waits for them, and re-layouts: 2.24 us -> 0 us
  other arithmetic: 0.7 us -> 0 us
    pallas_call x1, Pallas kernels: 48.7 us -> 46.6 us  [body(): pl.pallas_call(functools.partial(fused_kernel, n_req, n_pages, n_seq, n_t...]
    pallas_call x1, Pallas kernels: 6.2 us -> 4.14 us  [body(): pl.pallas_call(accept_kernel, out_shape=(jax.ShapeDtypeStruct((2, n_req,...]
    unnamed x1 -> x0, local copies, waits for them, and re-layouts: 1.47 us -> none
    eq x1 -> x0, local copies, waits for them, and re-layouts: 0.77 us -> none  [body(): page_table.reshape(1, -1) == slots[:, None]]
    reduce_sum x1 -> x0, other arithmetic: 0.69 us -> none  [body(): jnp.sum(jnp.where(page_table.reshape(1, -1) == slots[:, None], number[Non...]
where the time goes in v3:
time: 51.8 us; the launch traced here: 51.4 us
  Pallas kernels  50.7 us (98%)
  between operations  0.64 us (1%)
    pallas_call x1, Pallas kernels, body(): pl.pallas_call(functools.partial(fused_kernel, n_req, n_pages, n_seq, n_t...  46.6 us
    pallas_call x1, Pallas kernels, body(): pl.pallas_call(accept_kernel, out_shape=(jax.ShapeDtypeStruct((2, n_req,...  4.14 us

profile of v3, /device:TPU:11, one launch (start us, length us, event | category | flops | bytes accessed | tf_op | source)
XLA Modules:
  0.0 51.4 jit_solution(2523577481196090144)
XLA Ops:
  0.6 46.6 %shard_map.95 = (bf16[32,1024]{1,0:T(8,128)(2,1)}, bf16[8,2,32,1024]{3,2,1,0:T(8,128)(2,1)}) custom-call(s32[4,32]{1,0:T(4,128)} %table.1, s32[4]{0:T(128)} %cache_len.1, s32[8,32,64]{2,1,0:T(8,128)} %bitcast.3, bf16[32,1024]{1,0:T(8,128)(2,1)} %q.1, bf16[2,32,1024]{2,1,0:T(8,128)(2,1)} %kv.1, bf16[2,16,128,1024]{3,2,1,0:T(8,128)(2,1)} %pool.1, ...), custom_call_target="tpu_custom_call" | custom-call | flops 10000000000 | bytes 30000000 | tf_op jit(solution)/shard_map/pallas_call | solution.py:307
  47.2 4.1 %shard_map.96 = (bf16[2,4,128,1024]{3,2,1,0:T(8,128)(2,1)}, bf16[32,1024]{1,0:T(8,128)(2,1)}) custom-call(s32[4,64]{1,0:T(4,128)} %rows_ref.1, bf16[4,2,2,32,1024]{4,3,2,1,0:T(8,128)(2,1)} %bitcast.2, bf16[32,1024]{1,0:T(8,128)(2,1)} %get-tuple-element.7.layer), custom_call_target="tpu_custom_call" | custom-call | tf_op jit(solution)/shard_map/pallas_call | solution.py:344

commit v4 on v3

--- a/solution.py
+++ b/solution.py
@@ -76,11 +76,6 @@
         send(q, block(me), qsem.at[d - 1], qrsem.at[me], {"seq": across(d)})
     for d in range(1, group):
         send(q, block(me), qsem.at[n_req - 2 + d], qrsem.at[me], {"seq": other(d)})
-    for d in range(1, group):
-        send(kv, kva.at[me], cssem.at[n_req - 2 + d], crsem.at[me], {"seq": other(d)})
-    for d in range(n_req - 1, 0, -1):
-        send(kv, kva.at[me], cssem.at[d - 1], crsem.at[me], {"seq": across(d)})
-
     def q_arrived(b):
         remote(q, block(b), qsem.at[0], qrsem.at[b], {"seq": other(1)}).wait_recv()
 
@@ -107,6 +102,10 @@
         for d in range(1, group):
             send(block(b), block(b), fsem.at[(e - 1) * (group - 1) + d - 1], qrsem.at[b],
                  {"seq": other(d)})
+    for d in range(1, group):
+        send(kv, kva.at[me], cssem.at[n_req - 2 + d], crsem.at[me], {"seq": other(d)})
+    for d in range(n_req - 1, 0, -1):
+        send(kv, kva.at[me], cssem.at[d - 1], crsem.at[me], {"seq": across(d)})
     for d in range(1, group):
         q_arrived(other(d))
         for e in range(1, n_req):

time: 51.8 us -> 51 us (0.985)
  Pallas kernels: 50.7 us -> 50.1 us
    pallas_call x1, Pallas kernels: 46.6 us -> 46 us  [body(): pl.pallas_call(functools.partial(fused_kernel, n_req, n_pages, n_seq, n_t...]
where the time goes in v4:
time: 51 us; the launch traced here: 50.7 us
  Pallas kernels  50.1 us (98%)
  between operations  0.64 us (1%)
    pallas_call x1, Pallas kernels, body(): pl.pallas_call(functools.partial(fused_kernel, n_req, n_pages, n_seq, n_t...  46 us
    pallas_call x1, Pallas kernels, body(): pl.pallas_call(accept_kernel, out_shape=(jax.ShapeDtypeStruct((2, n_req,...  4.15 us

profile of v4, /device:TPU:11, one launch (start us, length us, event | category | flops | bytes accessed | tf_op | source)
XLA Modules:
  0.0 50.7 jit_solution(6112176327007603784)
XLA Ops:
  0.6 46.0 %shard_map.95 = (bf16[32,1024]{1,0:T(8,128)(2,1)}, bf16[8,2,32,1024]{3,2,1,0:T(8,128)(2,1)}) custom-call(s32[4,32]{1,0:T(4,128)} %table.1, s32[4]{0:T(128)} %cache_len.1, s32[8,32,64]{2,1,0:T(8,128)} %bitcast.3, bf16[32,1024]{1,0:T(8,128)(2,1)} %q.1, bf16[2,32,1024]{2,1,0:T(8,128)(2,1)} %kv.1, bf16[2,16,128,1024]{3,2,1,0:T(8,128)(2,1)} %pool.1, ...), custom_call_target="tpu_custom_call" | custom-call | flops 10000000000 | bytes 30000000 | tf_op jit(solution)/shard_map/pallas_call | solution.py:306
  46.6 4.1 %shard_map.96 = (bf16[2,4,128,1024]{3,2,1,0:T(8,128)(2,1)}, bf16[32,1024]{1,0:T(8,128)(2,1)}) custom-call(s32[4,64]{1,0:T(4,128)} %rows_ref.1, bf16[4,2,2,32,1024]{4,3,2,1,0:T(8,128)(2,1)} %bitcast.2, bf16[32,1024]{1,0:T(8,128)(2,1)} %get-tuple-element.7.layer), custom_call_target="tpu_custom_call" | custom-call | tf_op jit(solution)/shard_map/pallas_call | solution.py:343

commit v5 on v4

--- a/solution.py
+++ b/solution.py
@@ -17,11 +17,11 @@
 NT = (((1,), (1,)), ((), ()))
 
 
-def fused_kernel(n_req, n_pages, n_seq, n_tp, group, table, cache_len, mask, q, kv, pool, weight,
-                 out, kva,
-                 qa, kbuf, vbuf, m_st, l_st, acc_st, part, stat, got, gstat, kg, wbuf, att, tree,
+def fused_kernel(n_req, n_pages, n_seq, n_tp, group, table, cache_len, mask, accepted, q, kv, pool, weight,
+                 out, acc_kv,
+                 kva, picked, zeros, qa, kbuf, vbuf, m_st, l_st, acc_st, part, stat, got, gstat, wbuf, att, tree,
                  pbuf, prbuf, last, code,
-                 qsem, qrsem, fsem, cssem, crsem, cfsem, lsem, ksem, vsem, gsem,
+                 qsem, qrsem, fsem, cssem, crsem, cfsem, lsem, ksem, vsem, osem, zsem,
                  asem, arsem, tsem, trsem, wsem, psem, prsem):
     me = lax.axis_index("seq")
     tp = lax.axis_index("tp")
@@ -90,6 +90,13 @@
         c = pltpu.make_async_copy(weight.at[:, pl.ds(t * out_w, out_w)], wbuf.at[t], wsem.at[t])
         c.start()
         loads.append(c)
+    zeros[...] = jnp.zeros(zeros.shape, zeros.dtype)
+    writes = []
+    for r in range(n_req):
+        for c in range(2):
+            writes.append(pltpu.make_async_copy(
+                zeros, acc_kv.at[c, r, pl.ds(n_draft, zeros.shape[0])], zsem.at[r, c]))
+            writes[-1].start()
     shape = table.shape
     number = (lax.broadcasted_iota(jnp.int32, shape, 0) * n_pages
               + lax.broadcasted_iota(jnp.int32, shape, 1) + 1)
@@ -185,21 +192,14 @@
     own_kv.wait()
     for d in range(1, group):
         kv_arrived(other(d))
-    tree_in = []
-    for g in range(group):
-        c = pltpu.make_async_copy(kva.at[grp * group + g], kg.at[g], gsem.at[g])
-        c.start()
-        tree_in.append(c)
-    for c in tree_in:
-        c.wait()
     allowed = mask[me] == 1
     mine = qa[grp, pl.ds(pl.multiple_of(inner * rows, rows), rows), :]
     tree_m = []
     tree_l = []
     for h in range(heads):
         cols = slice(h * HD, (h + 1) * HD)
-        keys = jnp.concatenate([kg[g, 0, :, cols] for g in range(group)], axis=0)
-        values = jnp.concatenate([kg[g, 1, :, cols] for g in range(group)], axis=0)
+        keys = jnp.concatenate([kva[grp * group + g, 0, :, cols] for g in range(group)], axis=0)
+        values = jnp.concatenate([kva[grp * group + g, 1, :, cols] for g in range(group)], axis=0)
         x = lax.dot_general(mine[:, cols], keys, NT, preferred_element_type=jnp.float32) * scale
         x = jnp.where(allowed, x, NEGATIVE)
         top = jnp.max(x, axis=1, keepdims=True)
@@ -239,6 +239,20 @@
         c.start()
         sent.append(c)
     total = jnp.dot(att[...], wbuf[tp], preferred_element_type=jnp.float32)
+    for d in range(1, group):
+        for e in range(1, n_req):
+            kv_arrived(lax.rem(grp + e, n_req) * group + lax.rem(inner + d, group))
+    for r in range(n_req):
+        pick = (lax.broadcasted_iota(jnp.int32, (n_draft, n_draft), 0)
+                == accepted[r:r + 1, :]).astype(jnp.bfloat16)
+        for c in range(2):
+            blocks = jnp.concatenate([kva[r * group + g, c] for g in range(group)], axis=0)
+            picked[r, c] = lax.dot_general(
+                pick, blocks, (((0,), (0,)), ((), ())),
+                preferred_element_type=jnp.float32).astype(jnp.bfloat16)
+            writes.append(pltpu.make_async_copy(
+                picked.at[r, c], acc_kv.at[c, r, pl.ds(0, n_draft)], osem.at[r, c]))
+            writes[-1].start()
     for d in range(1, n_tp):
         pltpu.make_async_remote_copy(
             src_ref=pbuf.at[d - 1], dst_ref=prbuf.at[d - 1], send_sem=psem.at[d - 1],
@@ -246,46 +260,24 @@
             device_id_type=MESH).wait_recv()
         total = total + prbuf[d - 1].astype(jnp.float32)
     out[...] = total.astype(out.dtype)
-    for d in range(1, group):
-        for e in range(1, n_req):
-            kv_arrived(lax.rem(grp + e, n_req) * group + lax.rem(inner + d, group))
     for e in range(1, n_req):
         for d in range(1, group):
             forward(e, d, False)
+    for c in writes:
+        c.wait()
     for c in sent:
         c.wait_send()
 
 
-def accept_kernel(rows_ref, kv, layer, out, layer_out, blocks, picked, zeros, isem, osem, zsem, lsem):
-    n_req, group, _, rows, width = kv.shape
-    n_draft = group * rows
-    copies = []
-
-    def copy(a, b, sem):
-        c = pltpu.make_async_copy(a, b, sem)
+def copy_kernel(accepted, layer, out, layer_out, sem):
+    halves, n_req = accepted.shape[:2]
+    copies = [pltpu.make_async_copy(layer, layer_out, sem.at[halves * n_req])]
+    for c in range(halves):
+        for r in range(n_req):
+            copies.append(pltpu.make_async_copy(
+                accepted.at[c, r], out.at[c, r], sem.at[c * n_req + r]))
+    for c in copies:
         c.start()
-        return c
-
-    loads = []
-    for r in range(n_req):
-        for c in range(2):
-            loads.append([copy(kv.at[r, g, c], blocks.at[r, c, pl.ds(g * rows, rows)],
-                               isem.at[r, c, g]) for g in range(group)])
-    copies.append(copy(layer, layer_out, lsem.at[0]))
-    zeros[...] = jnp.zeros(zeros.shape, zeros.dtype)
-    for r in range(n_req):
-        for c in range(2):
-            copies.append(copy(zeros, out.at[c, r, pl.ds(n_draft, zeros.shape[0])], zsem.at[r, c]))
-    for r in range(n_req):
-        pick = (lax.broadcasted_iota(jnp.int32, (n_draft, n_draft), 0)
-                == rows_ref[r:r + 1, :]).astype(jnp.bfloat16)
-        for c in range(2):
-            for load in loads[2 * r + c]:
-                load.wait()
-            picked[r, c] = lax.dot_general(
-                pick, blocks[r, c], (((0,), (0,)), ((), ())),
-                preferred_element_type=jnp.float32).astype(out.dtype)
-            copies.append(copy(picked.at[r, c], out.at[c, r, pl.ds(0, n_draft)], osem.at[r, c]))
     for c in copies:
         c.wait()
 
@@ -303,13 +295,16 @@
     bf16, f32 = jnp.bfloat16, jnp.float32
     dma = pltpu.SemaphoreType.DMA
 
-    layer, kv_all = pl.pallas_call(
+    layer, accepted_block = pl.pallas_call(
         functools.partial(fused_kernel, n_req, n_pages, n_seq, n_tp, group),
         out_shape=(jax.ShapeDtypeStruct((rows, out_w), bf16),
-                   jax.ShapeDtypeStruct((n_seq, 2, rows, width), bf16)),
-        in_specs=[VMEM, SMEM, VMEM, ANY, ANY, ANY, ANY],
+                   jax.ShapeDtypeStruct((2, n_req, page_len, width), bf16)),
+        in_specs=[VMEM, SMEM, VMEM, VMEM, ANY, ANY, ANY, ANY],
         out_specs=(VMEM, ANY),
-        scratch_shapes=[pltpu.VMEM((n_req, n_draft, width), bf16),
+        scratch_shapes=[pltpu.VMEM((n_seq, 2, rows, width), bf16),
+                        pltpu.VMEM((n_req, 2, n_draft, width), bf16),
+                        pltpu.VMEM((page_len - n_draft, width), bf16),
+                        pltpu.VMEM((n_req, n_draft, width), bf16),
                         pltpu.VMEM((n_slots, page_len, width), bf16),
                         pltpu.VMEM((n_slots, page_len, width), bf16),
                         pltpu.VMEM((n_slots + 1, heads, n_draft, HD), f32),
@@ -319,7 +314,6 @@
                         pltpu.VMEM((n_seq, rows, HD), f32),
                         pltpu.VMEM((n_seq, rows, width), bf16),
                         pltpu.VMEM((n_seq, rows, HD), f32),
-                        pltpu.VMEM((group, 2, rows, width), bf16),
                         pltpu.VMEM((n_tp, width, out_w), bf16),
                         pltpu.VMEM((rows, width), bf16),
                         pltpu.VMEM((rows, width), f32),
@@ -330,28 +324,25 @@
                         dma(((n_req - 1) * (group - 1),)),
                         dma((n_req + group - 2,)), dma((n_seq,)),
                         dma(((n_req - 1) * (group - 1),)),
-                        dma((4,)), dma((n_slots,)), dma((n_slots,)), dma((group,)),
+                        dma((4,)), dma((n_slots,)), dma((n_slots,)), dma((n_req, 2)), dma((n_req, 2)),
                         dma((n_seq - 1,)), dma((n_seq,)), dma((n_seq - 1,)), dma((n_seq,)),
                         dma((n_tp,)), dma((n_tp - 1,)), dma((n_tp - 1,))],
         compiler_params=pltpu.CompilerParams(collective_id=0, has_side_effects=True,
                                              vmem_limit_bytes=58 << 20),
         cost_estimate=pl.CostEstimate(flops=10 ** 10, bytes_accessed=3 * 10 ** 7,
                                       transcendentals=10 ** 6),
-    )(page_table, cache_len, tree_mask.reshape(n_seq, rows, n_draft), draft_q, draft_kv, kv_pool,
+    )(page_table, cache_len, tree_mask.reshape(n_seq, rows, n_draft), accepted_rows, draft_q, draft_kv, kv_pool,
       out_weight)
 
     accepted_kv, layer_out = pl.pallas_call(
-        accept_kernel,
+        copy_kernel,
         out_shape=(jax.ShapeDtypeStruct((2, n_req, page_len, width), bf16),
                    jax.ShapeDtypeStruct((rows, out_w), bf16)),
-        in_specs=[VMEM, ANY, ANY],
+        in_specs=[ANY, ANY],
         out_specs=(ANY, ANY),
-        scratch_shapes=[pltpu.VMEM((n_req, 2, n_draft, width), bf16),
-                        pltpu.VMEM((n_req, 2, n_draft, width), bf16),
-                        pltpu.VMEM((page_len - n_draft, width), bf16),
-                        dma((n_req, 2, group)), dma((n_req, 2)), dma((n_req, 2)), dma((1,))],
+        scratch_shapes=[dma((2 * n_req + 1,))],
         compiler_params=pltpu.CompilerParams(vmem_limit_bytes=58 << 20),
-    )(accepted_rows, kv_all.reshape(n_req, group, 2, rows, width), layer)
+    )(accepted_block, layer)
     return (layer_out, accepted_kv)
 
 

time: 51 us -> 114 us (2.24)
  Pallas kernels: 50.1 us -> 113 us
    pallas_call x1, Pallas kernels: 4.15 us -> 66.7 us  [body(): pl.pallas_call(copy_kernel, out_shape=(jax.ShapeDtypeStruct((2, n_req, pa...]
where the time goes in v5:
time: 114 us; the launch traced here: 113 us
  Pallas kernels  113 us (99%)
    pallas_call x1, Pallas kernels, body(): pl.pallas_call(copy_kernel, out_shape=(jax.ShapeDtypeStruct((2, n_req, pa...  66.7 us
    pallas_call x1, Pallas kernels, body(): pl.pallas_call(functools.partial(fused_kernel, n_req, n_pages, n_seq, n_t...  46.1 us

profile of v5, /device:TPU:11, one launch (start us, length us, event | category | flops | bytes accessed | tf_op | source)
XLA Modules:
  0.0 113.4 jit_solution(7216281847561698510)
XLA Ops:
  0.6 46.1 %shard_map.95 = (bf16[32,1024]{1,0:T(8,128)(2,1)}, bf16[2,4,128,1024]{3,2,1,0:T(8,128)(2,1)}) custom-call(s32[4,32]{1,0:T(4,128)} %table.1, s32[4]{0:T(128)} %cache_len.1, s32[8,32,64]{2,1,0:T(8,128)} %bitcast.1, s32[4,64]{1,0:T(4,128)} %accepted.1, bf16[32,1024]{1,0:T(8,128)(2,1)} %q.1, bf16[2,32,1024]{2,1,0:T(8,128)(2,1)} %kv.1, ...), custom_call_target="tpu_custom_call" | custom-call | flops 10000000000 | bytes 30000000 | tf_op jit(solution)/shard_map/pallas_call | solution.py:298
  46.7 66.7 %shard_map.96 = (bf16[2,4,128,1024]{3,2,1,0:T(8,128)(2,1)}, bf16[32,1024]{1,0:T(8,128)(2,1)}) custom-call(bf16[2,4,128,1024]{3,2,1,0:T(8,128)(2,1)} %get-tuple-element.6.accepted, bf16[32,1024]{1,0:T(8,128)(2,1)} %get-tuple-element.7.layer), custom_call_target="tpu_custom_call" | custom-call | tf_op jit(solution)/shard_map/pallas_call | solution.py:337

commit v6 on v5

--- a/solution.py
+++ b/solution.py
@@ -269,16 +269,20 @@
         c.wait_send()
 
 
-def copy_kernel(accepted, layer, out, layer_out, sem):
+def copy_kernel(accepted, layer, out, layer_out, held, held_layer, isem, osem):
     halves, n_req = accepted.shape[:2]
-    copies = [pltpu.make_async_copy(layer, layer_out, sem.at[halves * n_req])]
+    parts = [(layer, held_layer, layer_out)]
     for c in range(halves):
         for r in range(n_req):
-            copies.append(pltpu.make_async_copy(
-                accepted.at[c, r], out.at[c, r], sem.at[c * n_req + r]))
-    for c in copies:
+            parts.append((accepted.at[c, r], held.at[c, r], out.at[c, r]))
+    loads = [pltpu.make_async_copy(a, b, isem.at[i]) for i, (a, b, _) in enumerate(parts)]
+    stores = [pltpu.make_async_copy(b, c, osem.at[i]) for i, (_, b, c) in enumerate(parts)]
+    for c in loads:
         c.start()
-    for c in copies:
+    for load, store in zip(loads, stores):
+        load.wait()
+        store.start()
+    for c in stores:
         c.wait()
 
 
@@ -340,7 +344,9 @@
                    jax.ShapeDtypeStruct((rows, out_w), bf16)),
         in_specs=[ANY, ANY],
         out_specs=(ANY, ANY),
-        scratch_shapes=[dma((2 * n_req + 1,))],
+        scratch_shapes=[pltpu.VMEM((2, n_req, page_len, width), bf16),
+                        pltpu.VMEM((rows, out_w), bf16),
+                        dma((2 * n_req + 1,)), dma((2 * n_req + 1,))],
         compiler_params=pltpu.CompilerParams(vmem_limit_bytes=58 << 20),
     )(accepted_block, layer)
     return (layer_out, accepted_kv)

time: 114 us -> 49.3 us (0.43)
  Pallas kernels: 113 us -> 48.5 us
    pallas_call x1, Pallas kernels: 66.7 us -> 2.45 us  [body(): pl.pallas_call(copy_kernel, out_shape=(jax.ShapeDtypeStruct((2, n_req, pa...]
where the time goes in v6:
time: 49.3 us; the launch traced here: 49.2 us
  Pallas kernels  48.5 us (98%)
  between operations  0.64 us (1%)
    pallas_call x1, Pallas kernels, body(): pl.pallas_call(functools.partial(fused_kernel, n_req, n_pages, n_seq, n_t...  46.1 us
    pallas_call x1, Pallas kernels, body(): pl.pallas_call(copy_kernel, out_shape=(jax.ShapeDtypeStruct((2, n_req, pa...  2.45 us

profile of v6, /device:TPU:11, one launch (start us, length us, event | category | flops | bytes accessed | tf_op | source)
XLA Modules:
  0.0 49.2 jit_solution(4235893915167873522)
XLA Ops:
  0.6 46.1 %shard_map.95 = (bf16[32,1024]{1,0:T(8,128)(2,1)}, bf16[2,4,128,1024]{3,2,1,0:T(8,128)(2,1)}) custom-call(s32[4,32]{1,0:T(4,128)} %table.1, s32[4]{0:T(128)} %cache_len.1, s32[8,32,64]{2,1,0:T(8,128)} %bitcast.1, s32[4,64]{1,0:T(4,128)} %accepted.1, bf16[32,1024]{1,0:T(8,128)(2,1)} %q.1, bf16[2,32,1024]{2,1,0:T(8,128)(2,1)} %kv.1, ...), custom_call_target="tpu_custom_call" | custom-call | flops 10000000000 | bytes 30000000 | tf_op jit(solution)/shard_map/pallas_call | solution.py:302
  46.7 2.5 %shard_map.96 = (bf16[2,4,128,1024]{3,2,1,0:T(8,128)(2,1)}, bf16[32,1024]{1,0:T(8,128)(2,1)}) custom-call(bf16[2,4,128,1024]{3,2,1,0:T(8,128)(2,1)} %get-tuple-element.6.accepted, bf16[32,1024]{1,0:T(8,128)(2,1)} %get-tuple-element.7.layer), custom_call_target="tpu_custom_call" | custom-call | tf_op jit(solution)/shard_map/pallas_call | solution.py:341
